TPU v7x, 32 devices: a whole 2x2x4 slice. The times are simulated.
32 devices in a mesh: groups: 2 (over y), ctx: 4 (over z), fsdp: 2 (over x), head: 2 (over core).
Axes of the slice: x: 2, y: 2, z: 4, core: 2. Of those that a mesh axis runs over, the one named last changes fastest.
Arguments:
- hidden_in: bfloat16 [4, 512, 8192], P(('groups', 'fsdp'), 'ctx', 'head'), parts along dimension 0, may hold values from -8 to 8
- w_bc: bfloat16 [8192, 256], P('fsdp'), may hold values from -0.0625 to 0.0625
- x_in: bfloat16 [4, 512, 4096], P(('groups', 'fsdp'), 'ctx', 'head'), parts along dimension 0, may hold values from -6 to 6
- dt_raw: float32 [4, 512, 64], P(('groups', 'fsdp'), 'ctx', 'head'), parts along dimension 0, may hold values from -2 to 5
- decay_rate: float32 [64], P('head'), may hold values from 0.001171875 to 0.033
- conv_x: float32 [4, 4096], P(None, 'head'), may hold values from -3 to 3
- conv_bc: float32 [4, 256], replicated, may hold values from -3 to 3
- skip_gain: float32 [64], P('head'), may hold values from -10 to 10
- span_len: int32 [4, 4], P(('groups', 'fsdp')), parts along dimension 0, may hold values from 1 to 256, 512 in all within a row
- grad_y: bfloat16 [4, 512, 4096], P(('groups', 'fsdp'), 'ctx', 'head'), parts along dimension 0, may hold values from -6 to 6
Outputs:
- grad_x: bfloat16 [4, 512, 4096], P(('groups', 'fsdp'), 'ctx', 'head'), parts along dimension 0
- grad_u: bfloat16 [4, 512, 8192], P(('groups', 'fsdp'), 'ctx', 'head'), parts along dimension 0
- grad_dt: float32 [4, 512, 64], P(('groups', 'fsdp'), 'ctx', 'head'), parts along dimension 0
- grad_w: float32 [4, 4096, 256], P(('groups', 'head'), ('ctx', 'fsdp')), parts along dimension 0
There are 2 independent parts, one for each index of `groups`. A program takes and returns all parts, laid end to end along the dimension named above; an argument that names none is the same for every part. Nothing has to cross between parts.
Inputs may be any that keep to these rules, and one draw needn't show every extreme that they name: `span_len`: each list's spans lie end to end over its 512 tokens; each has 1 to 256 tokens and some span has exactly 256.
All inputs are finite; a program needn't handle non-finite values.
Results may differ from a plain program's by a relative error of at most 0.0057.
Values may be sent and summed in bfloat16 or wider, within the bound.
A program may use at most 128 MiB of HBM per device.

v0:
```python
import jax
import jax.numpy as jnp
from jax import lax
from jax.sharding import PartitionSpec as P

STATE = 128


exact_mode = lax.Precision.HIGHEST


def from_behind(block, axis, distance):
    devices = range(lax.axis_size(axis))
    route = [(i - distance, i) for i in devices if i - distance in devices]
    return lax.ppermute(block, axis, route)


def entering(array, axis, combine, identity, reverse):
    peers, mine = (lax.axis_size(axis), lax.axis_index(axis))
    everything = jax.tree.map(lambda part: lax.all_gather(part, axis), array)
    start = jax.tree.map(
        lambda part, zero: jnp.broadcast_to(jnp.asarray(zero, part.dtype), part.shape),
        array,
        identity,
    )

    def hop(k, before):
        at = peers - 1 - k if reverse else k
        reached = at > mine if reverse else at < mine
        new = combine(before, jax.tree.map(lambda part: part[at], everything))
        return jax.tree.map(lambda a, b: jnp.where(reached, a, b), new, before)

    return lax.fori_loop(0, peers, hop, start)


def causal_conv(values, conv_taps, segment):
    tok_rows = values.shape[0] - 3
    summed = jnp.zeros((tok_rows, values.shape[1]), jnp.float32)
    for offset in range(4):
        same_span = (segment[offset : offset + tok_rows] == segment[3:]).astype(jnp.float32)
        summed = (
            summed
            + conv_taps[offset][None, :] * values[offset : offset + tok_rows] * same_span[:, None]
        )
    return summed


def prepare(x_halo, bc_halo, raw_steps, segment, conv_x, conv_bc, decay_rate):
    x_conv = jax.nn.silu(causal_conv(x_halo, conv_x, segment))
    bc_conv = jax.nn.silu(causal_conv(bc_halo, conv_bc, segment))
    dt_soft = jax.nn.softplus(raw_steps)
    log_step = -dt_soft * decay_rate[None, :]
    return (x_conv, bc_conv[:, :STATE], bc_conv[:, STATE:], dt_soft, log_step)


def block_outputs(
    x_conv, b_state, c_state, dt_soft, log_step, start_state, segment, seg_before, skip_gain
):
    tok_rows = x_conv.shape[0]
    head_count = dt_soft.shape[1]
    x_heads = x_conv.reshape(tok_rows, head_count, -1)
    cumulative = jnp.cumsum(log_step, axis=0).T
    token_index = jnp.arange(tok_rows)
    within = (segment[:, None] == segment[None, :]) & (token_index[:, None] >= token_index[None, :])
    log_gap = cumulative[:, :, None] - cumulative[:, None, :]
    decay_table = jnp.exp(jnp.where(within[None], log_gap, -1e30))
    scores = jnp.dot(c_state, b_state.T, precision=exact_mode, preferred_element_type=jnp.float32)
    weighted = x_heads * dt_soft[:, :, None]
    intra_out = jnp.einsum(
        "hts,shp->thp", decay_table * scores[None], weighted, precision=exact_mode
    )
    alive_mask = (segment == seg_before).astype(jnp.float32)
    carried = jnp.exp(cumulative.T) * alive_mask[:, None]
    state_out = (
        jnp.einsum("tn,hpn->thp", c_state, start_state, precision=exact_mode) * carried[:, :, None]
    )
    result = intra_out + state_out + skip_gain[None, :, None] * x_heads
    return result.reshape(tok_rows, -1)


def block_ends(x_conv, b_state, dt_soft, log_step, segment, seg_before):
    tok_rows = x_conv.shape[0]
    head_count = dt_soft.shape[1]
    x_heads = x_conv.reshape(tok_rows, head_count, -1)
    cumulative = jnp.cumsum(log_step, axis=0)
    last_same = (segment == segment[-1]).astype(jnp.float32)
    toward = jnp.exp(cumulative[-1][None, :] - cumulative) * last_same[:, None]
    weighted = x_heads * (dt_soft * toward)[:, :, None]
    ends_state = jnp.einsum("shp,sn->hpn", weighted, b_state, precision=exact_mode)
    through = jnp.exp(cumulative[-1]) * (segment[-1] == seg_before).astype(jnp.float32)
    return (through, ends_state)


def combine_states(earlier, later):
    return (earlier[0] * later[0], later[0][:, None, None] * earlier[1] + later[1])


def on_device(
    hidden_in, w_bc, x_in, dt_raw, decay_rate, conv_x, conv_bc, skip_gain, span_len, grad_y
):
    tok_rows = x_in.shape[1]
    hidden = hidden_in[0]
    half_width = hidden.shape[1]
    w_full = lax.all_gather(w_bc, "fsdp", axis=0, tiled=True)
    w_half = lax.dynamic_slice_in_dim(w_full, lax.axis_index("head") * half_width, half_width, 0)
    partial_bc = jnp.dot(hidden, w_half, preferred_element_type=jnp.float32)
    bc_pre = lax.psum(partial_bc, "head").astype(jnp.bfloat16)
    x_local = x_in[0]
    rim_x, rim_bc = from_behind((x_local[tok_rows - 3 :], bc_pre[tok_rows - 3 :]), "ctx", 1)
    x_halo = jnp.concatenate([rim_x, x_local]).astype(jnp.float32)
    bc_halo = jnp.concatenate([rim_bc, bc_pre]).astype(jnp.float32)
    position = lax.axis_index("ctx") * tok_rows + jnp.arange(tok_rows + 3, dtype=jnp.int32) - 3
    span_ends = jnp.cumsum(span_len[0])
    counted = jnp.sum((span_ends[None, :] <= position[:, None]).astype(jnp.int32), axis=1)
    segment = jnp.where(position >= 0, counted, -1)
    own_seg = segment[3:]
    seg_before = segment[2]

    def prepare_local(x_vals, bc_vals, raw_vals):
        return prepare(x_vals, bc_vals, raw_vals, segment, conv_x, conv_bc, decay_rate)

    prepared, prep_pull = jax.vjp(prepare_local, x_halo, bc_halo, dt_raw[0])
    x_conv, b_state, c_state, dt_soft, log_step = prepared

    def ends_local(x_vals, b_vals, dt_vals, log_vals):
        return block_ends(x_vals, b_vals, dt_vals, log_vals, own_seg, seg_before)

    ends_pair, ends_pull = jax.vjp(ends_local, x_conv, b_state, dt_soft, log_step)
    through, local_end = ends_pair
    cotangent = grad_y[0].astype(jnp.float32)
    head_count = dt_soft.shape[1]
    cumulative = jnp.cumsum(log_step, axis=0)
    alive_mask = (own_seg == seg_before).astype(jnp.float32)
    carried = jnp.exp(cumulative) * alive_mask[:, None]
    weighted_cot = cotangent.reshape(tok_rows, head_count, -1) * carried[:, :, None]
    from_outputs = jnp.einsum("thp,tn->hpn", weighted_cot, c_state, precision=exact_mode)
    identity = (jnp.ones_like(through), jnp.zeros_like(local_end))
    start_pair = entering((through, local_end), "ctx", combine_states, identity, False)
    start_state = start_pair[1]
    grad_pair = entering((through, from_outputs), "ctx", combine_states, identity, True)
    end_grad = grad_pair[1]
    sub_rows = min(tok_rows, max(64, tok_rows // 4))

    def outputs_local(x_vals, b_vals, c_vals, dt_vals, log_vals, state_vals):
        pieces = []
        carry_state = state_vals
        before = seg_before
        for row_start in range(0, tok_rows, sub_rows):
            row_stop = row_start + sub_rows
            seg_part = own_seg[row_start:row_stop]
            pieces.append(
                block_outputs(
                    x_vals[row_start:row_stop],
                    b_vals[row_start:row_stop],
                    c_vals[row_start:row_stop],
                    dt_vals[row_start:row_stop],
                    log_vals[row_start:row_stop],
                    carry_state,
                    seg_part,
                    before,
                    skip_gain,
                )
            )
            if row_stop < tok_rows:
                through_part, end_part = block_ends(
                    x_vals[row_start:row_stop],
                    b_vals[row_start:row_stop],
                    dt_vals[row_start:row_stop],
                    log_vals[row_start:row_stop],
                    seg_part,
                    before,
                )
                carry_state = through_part[:, None, None] * carry_state + end_part
            before = seg_part[-1]
        return jnp.concatenate(pieces, axis=0)

    unused, out_pull = jax.vjp(
        outputs_local, x_conv, b_state, c_state, dt_soft, log_step, start_state
    )
    grad_xc, grad_bs, grad_cs, grad_dts, grad_ls, unused_state = out_pull(cotangent)
    through_cot = jnp.sum(end_grad * start_state, axis=(1, 2))
    end_x, end_b, end_dt, end_log = ends_pull((through_cot, end_grad))
    grad_xhalo, grad_bchalo, grad_raw = prep_pull(
        (grad_xc + end_x, grad_bs + end_b, grad_cs, grad_dts + end_dt, grad_ls + end_log)
    )
    back_x, back_bc = from_behind((grad_xhalo[:3], grad_bchalo[:3]), "ctx", -1)
    grad_xown = grad_xhalo[3:] + jnp.pad(back_x, ((tok_rows - 3, 0), (0, 0)))
    grad_bcown = grad_bchalo[3:] + jnp.pad(back_bc, ((tok_rows - 3, 0), (0, 0)))
    d_bcpre = lax.psum(grad_bcown, "head")
    d_bc = d_bcpre.astype(jnp.bfloat16)
    grad_hidden = jnp.dot(d_bc, w_half.T, preferred_element_type=jnp.float32).astype(jnp.bfloat16)
    grad_w = lax.psum_scatter(
        lax.dot_general(hidden, d_bc, (((0,), (0,)), ((), ())), preferred_element_type=jnp.float32),
        ("ctx", "fsdp"),
        scatter_dimension=0,
        tiled=True,
    )
    return (grad_xown.astype(jnp.bfloat16)[None], grad_hidden[None], grad_raw[None], grad_w[None])


def solution(mesh):
    return jax.shard_map(
        on_device,
        mesh=mesh,
        in_specs=(
            P(("groups", "fsdp"), "ctx", "head"),
            P("fsdp", None),
            P(("groups", "fsdp"), "ctx", "head"),
            P(("groups", "fsdp"), "ctx", "head"),
            P("head"),
            P(None, "head"),
            P(),
            P("head"),
            P(("groups", "fsdp"), None),
            P(("groups", "fsdp"), "ctx", "head"),
        ),
        out_specs=(
            P(("groups", "fsdp"), "ctx", "head"),
            P(("groups", "fsdp"), "ctx", "head"),
            P(("groups", "fsdp"), "ctx", "head"),
            P(("groups", "head"), ("ctx", "fsdp"), None),
        ),
        check_vma=False,
    )
```

profile of v0, /device:TPU:0, one launch (start us, length us, event | category | flops | bytes accessed | tf_op | source)
XLA Modules:
  0.0 407.1 jit_solution(2110445724281553024)
XLA Ops:
  13.3 55.8 %all-gather.7.cloned.1.call-done = bf16[8192,256]{1,0:T(8,128)(2,1)} async-done(((bf16[4096,256]{1,0:T(8,128)(2,1)}), bf16[8192,256]{1,0:T(8,128)(2,1)}) %all-gather.7.cloned.1.call-update) | async-done | bytes 4194320 | tf_op jit(solution)/shard_map/all_gather | solution.py:104
  69.1 2.0 fusion.8
  71.1 3.8 all-reduce.32
  75.0 3.4 collective-permute-start
  83.3 4.2 %collective-permute-start.1 = (bf16[3,2048]{1,0:T(4,128)(2,1)S(1)}, bf16[3,2048]{1,0:T(4,128)(2,1)S(1)}, u32[]{:S(2)}, u32[]{:S(2)}) collective-permute-start(bf16[3,2048]{1,0:T(4,128)(2,1)S(1)} %slice_bitcast_fusion.5), channel_id=1, source_target_pairs={{0,4},{4,8},{8,12},{1,5},{5,9},{9,13},{2,6},{6,10},{10,14},{3,7},{... | collective-permute-start | bytes 36872 | tf_op jit(solution)/shard_map/ppermute | solution.py:15
  101.5 12.1 %all-gather.2 = f32[4,1,32]{2,1,0:T(1,128)} all-gather(f32[1,1,32]{2,1,0:T(1,128)} %get-tuple-element.358), channel_id=1, replica_groups=mesh['groups'=2,'ctx'=4,'fsdp'=2,'head'=2] {'ctx'}, dimensions={0}, use_global_device_ids=true | all-gather | bytes 640 | tf_op jit(solution)/shard_map/all_gather | solution.py:20
  114.4 2.7 compare_convert_fusion
  118.4 2.9 fusion.121
  122.4 2.3 copy.262
  124.7 2.4 copy.260
  128.1 3.3 convolution_bitcast_fusion.3
  131.4 32.9 %all-gather.9.cloned.1.call-done = f32[128,64,128]{2,1,0:T(8,128)} async-done(((f32[32,64,128]{2,1,0:T(8,128)}), f32[128,64,128]{2,1,0:T(8,128)}) %all-gather.9.cloned.1.call-update) | async-done | bytes 4194320 | tf_op jit(solution)/shard_map/all_gather | solution.py:20
  164.3 6.0 %while.30 = (s32[]{:T(128)}, f32[32,64,128]{2,1,0:T(8,128)S(1)}, s32[]{:T(128)}, f32[4,32]{1,0:T(4,128)S(1)}, f32[4,32,64,128]{3,2,1,0:T(8,128)}, /*index=5*/s32[]{:T(128)}, s32[]{:T(128)}, s32[]{:T(128)}, s32[]{:T(128)}) while((s32[]{:T(128)}, f32[32,64,128]{2,1,0:T(8,128)S(1)}, s32[]{:T(128)}, f32[4,32]{1,0:T(4,128)S(1)}, ...), condition=%wide.region_7.8_spmd.clone, body=%wide.region_6.7_spmd.clone.sunk | while | flops 1048584 | bytes 3146287 | solution.py:33
  170.3 74.9 %all-gather.11.cloned.1.call-done = f32[128,64,128]{2,1,0:T(8,128)} async-done(((f32[32,64,128]{2,1,0:T(8,128)}), f32[128,64,128]{2,1,0:T(8,128)}) %all-gather.11.cloned.1.call-update) | async-done | bytes 4194320 | tf_op jit(solution)/shard_map/all_gather | solution.py:20
  245.2 6.2 %while.31 = (s32[]{:T(128)}, f32[32,64,128]{2,1,0:T(8,128)S(1)}, s32[]{:T(128)}, f32[4,32]{1,0:T(4,128)S(1)}, f32[4,32,64,128]{3,2,1,0:T(8,128)}, /*index=5*/s32[]{:T(128)}, s32[]{:T(128)}) while((s32[]{:T(128)}, f32[32,64,128]{2,1,0:T(8,128)S(1)}, s32[]{:T(128)}, f32[4,32]{1,0:T(4,128)S(1)}, f32[4,32,64,128]{3,2,1,0:T(8,128)}, ...), condition=%wide.region_9.10_spmd.clone, body=%wide.region_8.9_spmd.clone.sunk | while | flops 1048580 | bytes 3146225 | solution.py:33
  251.3 3.8 multiply_reduce_fusion.2
  257.9 3.8 multiply_reduce_fusion.1
  263.8 2.3 convolution_add_fusion
  267.7 2.5 convolution_bitcast_fusion.8
  273.3 3.7 fusion.42
  278.4 2.5 convolution_bitcast_fusion.6
  280.9 3.2 multiply_reduce_fusion.3
  289.0 3.2 fusion.40
  299.9 4.1 %collective-permute-done.3 = f32[3,256]{1,0:T(4,128)S(1)} collective-permute-done((f32[3,256]{1,0:T(4,128)S(1)}, f32[3,256]{1,0:T(4,128)S(1)}, u32[]{:S(2)}, u32[]{:S(2)}) %collective-permute-start.3) | collective-permute-done | bytes 3104 | tf_op jit(solution)/shard_map/ppermute | solution.py:15
  304.0 4.1 %all-reduce.33 = bf16[128,256]{1,0:T(8,128)(2,1)S(1)} all-reduce(f32[128,256]{1,0:T(8,128)S(1)} %slice_add_fusion.1), channel_id=1, replica_groups=mesh['groups'=2,'ctx'=4,'fsdp'=2,'head'=2] {'head'}, use_global_device_ids=true, to_apply=%region_12.13 | all-reduce | flops 32768 | bytes 196608 | tf_op jit(solution)/shard_map/psum | solution.py:189
  308.2 2.8 convolution_bitcast_fusion
  319.6 3.8 multiply_reduce_fusion.5
  323.4 2.5 copy.245
  332.0 2.2 broadcast_multiply_fusion.2
  338.7 3.6 collective-permute-done.2
  343.2 55.2 %reduce-scatter.2.cloned.1.call-done = f32[512,256]{0,1:T(8,128)} async-done(((f32[4096,256]{0,1:T(8,128)}), f32[512,256]{0,1:T(8,128)}) %reduce-scatter.2.cloned.1.call-update) | async-done | bytes 524304 | tf_op jit(solution)/shard_map/reduce_scatter | solution.py:192
  398.5 2.0 copy.277
  (281 shorter events, 81.1 us)
Async XLA Ops:
  7.2 61.9 %copy-start = (bf16[1,128,4096]{2,1,0:T(8,128)(2,1)S(1)}, bf16[1,128,4096]{2,1,0:T(8,128)(2,1)}, u32[]{:S(2)}) copy-start(bf16[1,128,4096]{2,1,0:T(8,128)(2,1)} %param.14) | copy-start | bytes 3145732
  7.2 61.9 %all-gather.7.cloned.1.call-start = ((), (), s32[]{:S(2)}) async-start(), calls=%async_computation.1 | async-start | bytes 6291456 | tf_op jit(solution)/shard_map/all_gather | solution.py:104
  7.9 70.5 %copy-start.76 = (f32[4,256]{1,0:T(4,128)S(1)}, f32[4,256]{1,0:T(4,128)}, u32[]{:S(2)}) copy-start(f32[4,256]{1,0:T(4,128)} %param.20) | copy-start | bytes 12292
  8.0 156.3 %all-gather.9.cloned.1.call-start = ((), (), s32[]{:S(2)}) async-start(), calls=%async_computation.3 | async-start | bytes 5242880 | tf_op jit(solution)/shard_map/all_gather | solution.py:20
  10.3 68.3 %copy-start.18 = (bf16[1,128,2048]{2,1,0:T(8,128)(2,1)S(1)}, bf16[1,128,2048]{2,1,0:T(8,128)(2,1)}, u32[]{:S(2)}) copy-start(bf16[1,128,2048]{2,1,0:T(8,128)(2,1)} %param.23) | copy-start | bytes 1572868
  11.9 66.5 %copy-start.71 = (f32[128]{0:T(128)}, f32[128]{0:T(128)S(1)}, u32[]{:S(2)}) copy-start(f32[128]{0:T(128)S(1)} %get-tuple-element.379) | copy-start | bytes 1540
  11.9 77.2 %copy-start.53 = (f32[128]{0:T(128)}, f32[128]{0:T(128)S(1)}, u32[]{:S(2)}) copy-start(f32[128]{0:T(128)S(1)} %get-tuple-element.380) | copy-start | bytes 1540
  11.9 77.2 %copy-start.56 = (f32[128]{0:T(128)}, f32[128]{0:T(128)S(1)}, u32[]{:S(2)}) copy-start(f32[128]{0:T(128)S(1)} %get-tuple-element.381) | copy-start | bytes 1540
  11.9 77.2 %copy-start.59 = (f32[128]{0:T(128)}, f32[128]{0:T(128)S(1)}, u32[]{:S(2)}) copy-start(f32[128]{0:T(128)S(1)} %get-tuple-element.383) | copy-start | bytes 1540
  12.6 65.9 %copy-start.70 = (f32[32]{0:T(128)}, f32[32]{0:T(128)S(1)}, u32[]{:S(2)}) copy-start(f32[32]{0:T(128)S(1)} %get-tuple-element.357) | copy-start | bytes 388
  75.0 4.7 %collective-permute-start = (bf16[3,256]{1,0:T(4,128)(2,1)S(1)}, bf16[3,256]{1,0:T(4,128)(2,1)S(1)}, u32[]{:S(2)}, u32[]{:S(2)}) collective-permute-start(bf16[3,256]{1,0:T(4,128)(2,1)S(1)} %slice.219), channel_id=1, source_target_pairs={{0,4},{4,8},{8,12},{1,5},{5,9},{9,13},{2,6},{6,10},{10,14},{3,7},{... | collective-permute-start | bytes 4616 | tf_op jit(solution)/shard_map/ppermute | solution.py:15
  78.9 8.6 %copy-start.50 = (f32[4,2048]{1,0:T(4,128)S(1)}, f32[4,2048]{1,0:T(4,128)}, u32[]{:S(2)}) copy-start(f32[4,2048]{1,0:T(4,128)} %param.19) | copy-start | bytes 98308
  80.5 8.5 %copy-start.20 = (bf16[1,128,2048]{2,1,0:T(8,128)(2,1)S(1)}, bf16[1,128,2048]{2,1,0:T(8,128)(2,1)}, u32[]{:S(2)}) copy-start(bf16[1,128,2048]{2,1,0:T(8,128)(2,1)} %param.16) | copy-start | bytes 1572868
  82.5 162.6 %all-gather.11.cloned.1.call-start = ((), (), s32[]{:S(2)}) async-start(), calls=%async_computation.4 | async-start | bytes 5242880 | tf_op jit(solution)/shard_map/all_gather | solution.py:20
  83.3 5.6 %collective-permute-start.1 = (bf16[3,2048]{1,0:T(4,128)(2,1)S(1)}, bf16[3,2048]{1,0:T(4,128)(2,1)S(1)}, u32[]{:S(2)}, u32[]{:S(2)}) collective-permute-start(bf16[3,2048]{1,0:T(4,128)(2,1)S(1)} %slice_bitcast_fusion.5), channel_id=1, source_target_pairs={{0,4},{4,8},{8,12},{1,5},{5,9},{9,13},{2,6},{6,10},{10,14},{3,7},{... | collective-permute-start | bytes 36872 | tf_op jit(solution)/shard_map/ppermute | solution.py:15
  93.2 305.3 %reduce-scatter.2.cloned.1.call-start = ((), (), s32[]{:S(2)}) async-start(), calls=%async_computation.2 | async-start | bytes 4718592 | tf_op jit(solution)/shard_map/reduce_scatter | solution.py:192
  94.7 26.6 %copy-start.26 = (f32[64,32]{0,1:T(8,128)}, f32[64,32]{0,1:T(8,128)S(1)}, u32[]{:S(2)}) copy-start(f32[64,32]{0,1:T(8,128)S(1)} %copy.246) | copy-start | bytes 24580
  95.7 32.4 %copy-start.52 = (f32[32,64]{1,0:T(8,128)}, f32[32,64]{1,0:T(8,128)S(1)}, u32[]{:S(2)}) copy-start(f32[32,64]{1,0:T(8,128)S(1)} %copy.249) | copy-start | bytes 24580
  118.4 9.7 %copy-start.72 = (pred[64,64]{0,1:T(8,128)(4,1)}, pred[64,64]{0,1:T(8,128)(4,1)S(1)}, u32[]{:S(2)}) copy-start(pred[64,64]{0,1:T(8,128)(4,1)S(1)} %fusion.90) | copy-start | bytes 12292
  118.4 139.4 %copy-start.24 = (f32[64,32]{0,1:T(8,128)}, f32[64,32]{0,1:T(8,128)S(1)}, u32[]{:S(2)}) copy-start(f32[64,32]{0,1:T(8,128)S(1)} %exponential_multiply_fusion.2) | copy-start | bytes 24580
  124.7 39.5 %copy-start.78 = (f32[4,1,32]{2,1,0:T(1,128)S(1)}, f32[4,1,32]{2,1,0:T(1,128)}, u32[]{:S(2)}) copy-start(f32[4,1,32]{2,1,0:T(1,128)} %all-gather.2) | copy-start | bytes 1540
  127.3 37.0 %copy-start.49 = (f32[64,64]{0,1:T(8,128)}, f32[64,64]{0,1:T(8,128)S(1)}, u32[]{:S(2)}) copy-start(f32[64,64]{0,1:T(8,128)S(1)} %fusion.98) | copy-start | bytes 49156
  273.2 7.6 %copy-start.8 = (f32[1,64,2048]{1,2,0:T(8,128)S(1)}, f32[1,64,2048]{1,2,0:T(8,128)}, u32[]{:S(2)}) copy-start(f32[1,64,2048]{1,2,0:T(8,128)} %get-tuple-element.344) | copy-start | bytes 1572868
  273.2 7.6 %copy-start.19 = (f32[64,32,64]{0,2,1:T(8,128)S(1)}, f32[64,32,64]{0,2,1:T(8,128)}, u32[]{:S(2)}) copy-start(f32[64,32,64]{0,2,1:T(8,128)} %convolution_bitcast_fusion.3) | copy-start | bytes 1572868
  273.3 7.6 %copy-start.45 = (f32[64,32]{0,1:T(8,128)S(1)}, f32[64,32]{0,1:T(8,128)}, u32[]{:S(2)}) copy-start(f32[64,32]{0,1:T(8,128)} %copy.254) | copy-start | bytes 24580
  273.3 7.6 %copy-start.79 = (f32[32]{0:T(128)S(1)}, f32[32]{0:T(128)}, u32[]{:S(2)}) copy-start(f32[32]{0:T(128)} %param.21) | copy-start | bytes 388
  298.5 5.5 %collective-permute-start.3 = (f32[3,256]{1,0:T(4,128)S(1)}, f32[3,256]{1,0:T(4,128)S(1)}, u32[]{:S(2)}, u32[]{:S(2)}) collective-permute-start(f32[3,256]{1,0:T(4,128)S(1)} %pad_add_fusion.6), channel_id=1, source_target_pairs={{4,0},{8,4},{12,8},{5,1},{9,5},{13,9},{6,2},{10,6},{14,10},{7,3},{... | collective-permute-start | bytes 9224 | tf_op jit(solution)/shard_map/ppermute | solution.py:15
  311.0 8.6 %copy-start.2 = (f32[1,64,2048]{1,2,0:T(8,128)S(1)}, f32[1,64,2048]{1,2,0:T(8,128)}, u32[]{:S(2)}) copy-start(f32[1,64,2048]{1,2,0:T(8,128)} %get-tuple-element.343) | copy-start | bytes 1572868
  311.0 8.6 %copy-start.29 = (f32[64,64]{0,1:T(8,128)S(1)}, f32[64,64]{0,1:T(8,128)}, u32[]{:S(2)}) copy-start(f32[64,64]{0,1:T(8,128)} %fusion.93) | copy-start | bytes 49156
  319.5 7.4 %copy-start.46 = (f32[64,32]{0,1:T(8,128)S(1)}, f32[64,32]{0,1:T(8,128)}, u32[]{:S(2)}) copy-start(f32[64,32]{0,1:T(8,128)} %get-tuple-element.385) | copy-start | bytes 24580
  319.6 8.4 %copy-start.32 = (f32[64,32]{1,0:T(8,128)S(1)}, f32[64,32]{1,0:T(8,128)}, u32[]{:S(2)}) copy-start(f32[64,32]{1,0:T(8,128)} %get-tuple-element.348) | copy-start | bytes 24580
  334.7 7.7 %collective-permute-start.2 = (f32[3,2048]{1,0:T(4,128)S(1)}, f32[3,2048]{1,0:T(4,128)S(1)}, u32[]{:S(2)}, u32[]{:S(2)}) collective-permute-start(f32[3,2048]{1,0:T(4,128)S(1)} %pad_add_fusion.4), channel_id=1, source_target_pairs={{4,0},{8,4},{12,8},{5,1},{9,5},{13,9},{6,2},{10,6},{14,10},{7,3},{... | collective-permute-start | bytes 73736 | tf_op jit(solution)/shard_map/ppermute | solution.py:15
  (57 other events, 206.1 us)
Sparse Core Ops, SparseCore 0:
  9.6 59.4 all-gather.6
  82.6 81.5 all-gather.8
  165.8 79.2 all-gather.10
  311.1 87.3 reduce-scatter.1
where the time goes:
time: 409 us; the launch traced here: 407 us
  waiting for transfers between devices  228 us (56%)
  matrix products  52 us (13%)
  other arithmetic  40.1 us (10%)
  local copies, waits for them, and re-layouts  38.2 us (9%)
  blocking collectives  20.1 us (5%)
  between operations  17.4 us (4%)
  starting transfers between devices  10.6 us (3%)
    all_gather x2, waiting for transfers between devices, entering(): everything = jax.tree.map(lambda part: lax.all_gather(part, axis), array)  108 us
    all_gather x1, waiting for transfers between devices, on_device(): w_full = lax.all_gather(w_bc, 'fsdp', axis=0, tiled=True)  55.8 us
    reduce_scatter x1, waiting for transfers between devices, on_device(): lax.psum_scatter(lax.dot_general(hidden, d_bc, (((0,), (0,)), ((), ())),...  55.2 us
    dot_general x6, matrix products, block_ends(): jnp.einsum('shp,sn->hpn', weighted, b_state, precision=exact_mode)  15.6 us
    dot_general x4, matrix products, block_outputs(): jnp.einsum('hts,shp->thp', decay_table * scores[None], weighted, precisio...  14.1 us
    all_gather x1, blocking collectives, entering(): everything = jax.tree.map(lambda part: lax.all_gather(part, axis), array)  12.1 us
    select_n x8, other arithmetic, hop(): return jax.tree.map(lambda a, b: jnp.where(reached, a, b), new, before)  11.7 us
    dot_general x5, matrix products, block_outputs(): jnp.einsum('tn,hpn->thp', c_state, start_state, precision=exact_mode)  11.4 us
  transfers between devices with their start and end apart: 8, of which 8 were waited for; matrix products, arithmetic and copies ran while one was open for 16% of the time, Pallas kernels for 0%

commit v1 on v0

v1 whole, which is shorter than its diff:
```python
import jax
import jax.numpy as jnp
from jax import lax
from jax.experimental import pallas as pl
from jax.experimental.pallas import tpu as pltpu
from jax.sharding import PartitionSpec as P

STATE = 128
HEAD = 64
MOST = 256
BF = jnp.bfloat16
F32 = jnp.float32
EXACT = lax.Precision.HIGHEST


def shifted(block, axis, distance):
    devices = range(lax.axis_size(axis))
    route = [(i - distance, i) for i in devices if i - distance in devices]
    return lax.ppermute(block, axis, route)


def dot(a, b, ca, cb, precision=None):
    return lax.dot_general(
        a, b, (((ca,), (cb,)), ((), ())), precision=precision, preferred_element_type=F32
    )


def ssm_kernel(
    x2, x1, x0, g0, g1, g2, b2, b1, b0, b3, b4, raw_ref, info_ref, segrow_ref,
    decay_ref, skip_ref, tapx_ref, tapb_ref,
    dx_ref, tail_ref, rim_ref, dbc_ref, rimbc_ref, ddt_ref,
    masks, bias_ref, s_ref, cols_a, cols_b, cum_rows, bprev, cnext, bown, cown,
    silu_bc, d_s, d_b, d_c, acc,
):
    T = x0.shape[0]
    pairs = x0.shape[1] // 128
    lane = lax.broadcasted_iota(jnp.int32, (T, 128), 1)
    row = lax.broadcasted_iota(jnp.int32, (T, 128), 0)
    low = lane < HEAD
    group = lane // 32
    info = info_ref[...]
    for k in range(3):
        masks[k] = jnp.broadcast_to(info[: 3 * T, k : k + 1], (3 * T, 128))

    def col(block, k):
        return info[block * T : (block + 1) * T, k : k + 1]

    tri = (row >= lane).astype(F32)
    decay = decay_ref[...]
    dts, cums, carried, toward = [], [], [], []
    for j in range(5):
        raw = raw_ref[j * T : (j + 1) * T, :]
        dt = jnp.maximum(raw, 0.0) + jnp.log1p(jnp.exp(-jnp.abs(raw)))
        cum = dot(tri, -dt * decay, 1, 0, EXACT)
        dts.append(dt)
        cums.append(cum)
        carried.append(jnp.exp(cum) * col(j, 3))
        toward.append(jnp.exp(cum[T - 1 :, :] - cum) * col(j, 4))
    a1 = dts[1] * toward[1]
    a2 = dts[0] * toward[0] * carried[1][T - 1 :, :]
    c1 = carried[3]
    c2 = carried[4] * carried[3][T - 1 :, :]

    def packed(p, q, r, s):
        return jnp.where(group == 0, p, jnp.where(group == 1, q, jnp.where(group == 2, r, s)))

    cols_a[...] = packed(dts[2], cums[2], carried[2], toward[2])
    cols_b[...] = packed(a2, a1, c1, c2)
    cum_rows[...] = cums[2].T
    same = col(2, 5) == segrow_ref[...]
    bias_ref[...] = jnp.where(same & (row >= lane), 0.0, -1e30)

    taps_b = tapb_ref[...]
    bc = jnp.concatenate([b2[...], b1[...], b0[...], b3[...], b4[...]]).astype(F32)
    pre_bc = taps_b[3:4, :] * bc
    for k in range(3):
        pre_bc += taps_b[k : k + 1, :] * pltpu.roll(bc, 3 - k, 0) * info[:, k : k + 1]
    sig_bc = jax.nn.sigmoid(pre_bc)
    conv_bc = pre_bc * sig_bc
    own_sig = sig_bc[2 * T : 3 * T]
    silu_bc[...] = own_sig * (1.0 + pre_bc[2 * T : 3 * T] * (1.0 - own_sig))
    bprev[...] = conv_bc[: 2 * T, :STATE].astype(BF)
    cnext[...] = conv_bc[3 * T :, STATE:].astype(BF)
    bown[...] = conv_bc[2 * T : 3 * T, :STATE]
    cown[...] = conv_bc[2 * T : 3 * T, STATE:]
    s_ref[...] = dot(cown[...], bown[...], 1, 1, EXACT)
    d_s[...] = jnp.zeros_like(d_s)
    d_b[...] = jnp.zeros_like(d_b)
    d_c[...] = jnp.zeros_like(d_c)
    acc[...] = jnp.zeros_like(acc)

    def pair(i, carry):
        at = pl.ds(pl.multiple_of(i * 128, 128), 128)
        ca = pltpu.roll(cols_a[...], (128 - 2 * i) % 128, 1)
        cb = pltpu.roll(cols_b[...], (128 - 2 * i) % 128, 1)

        def wide(c, q):
            return jnp.where(low, c[:, 32 * q : 32 * q + 1], c[:, 32 * q + 1 : 32 * q + 2])

        def tall(c, q):
            return c[:, 32 * q : 32 * q + 1], c[:, 32 * q + 1 : 32 * q + 2]

        taps = tapx_ref[:, at]
        xe = jnp.concatenate([x2[:, at], x1[:, at], x0[:, at]]).astype(F32)
        pre = taps[3:4, :] * xe
        for k in range(3):
            pre += taps[k : k + 1, :] * pltpu.roll(xe, 3 - k, 0) * masks[k]
        sig = jax.nn.sigmoid(pre)
        xc = pre * sig
        xown = xc[2 * T :]
        sown = sig[2 * T :]
        dsilu = sown * (1.0 + pre[2 * T :] * (1.0 - sown))
        dt_w = wide(ca, 0)
        toward_w = wide(ca, 3)
        xw = jnp.concatenate([xc[:T] * wide(cb, 0), xc[T : 2 * T] * wide(cb, 1)]).astype(BF)
        start = dot(xw, bprev[...], 0, 0)
        gw = jnp.concatenate(
            [g1[:, at].astype(F32) * wide(cb, 2), g2[:, at].astype(F32) * wide(cb, 3)]
        ).astype(BF)
        end_grad = dot(gw, cnext[...], 0, 0)
        start_b = start.astype(BF)
        end_b = end_grad.astype(BF)
        gy = g0[:, at].astype(F32)
        gg = jnp.concatenate([jnp.where(low, gy, 0.0), jnp.where(low, 0.0, gy)]).astype(BF)
        xt = xown * dt_w
        xt_b = xt.astype(BF)
        xx = jnp.concatenate([jnp.where(low, xt, 0.0), jnp.where(low, 0.0, xt)]).astype(BF)
        d_m = dot(gg, xt_b, 1, 1)
        cum_a, cum_b = tall(ca, 1)
        bias = bias_ref[...]
        decay_t = jnp.concatenate(
            [
                jnp.exp(cum_a - cum_rows[pl.ds(2 * i, 1), :] + bias),
                jnp.exp(cum_b - cum_rows[pl.ds(2 * i + 1, 1), :] + bias),
            ]
        )
        s_all = s_ref[...]
        s_two = jnp.concatenate([s_all, s_all])
        ls = decay_t * s_two
        ldm = decay_t * d_m
        d_s[...] += ldm[:T] + ldm[T:]
        d_x = dot(ls.astype(BF), gg, 0, 0)
        car = jnp.concatenate(tall(ca, 2))
        tow = jnp.concatenate(tall(ca, 3))
        c_u = car * dot(gg, start_b, 1, 0)
        d_c[...] += c_u[:T] + c_u[T:]
        c_own = cown[...]
        c_two = jnp.concatenate([c_own, c_own])
        r = jnp.sum(ldm * s_two + c_u * c_two, axis=1, keepdims=True)
        t_v = tow * dot(xx, end_b, 1, 0)
        d_b[...] += t_v[:T] + t_v[T:]
        d_xe = dot(bown[...].astype(BF), end_b, 1, 1) * toward_w
        d_xt = d_x + d_xe
        prod = xown * d_xt
        q_a = jnp.sum(jnp.where(low, prod, 0.0), axis=1, keepdims=True)
        q_b = jnp.sum(jnp.where(low, 0.0, prod), axis=1, keepdims=True)
        ends = jnp.sum(xt * d_xe, axis=0, keepdims=True)
        inner = end_grad * start
        low_row = low[:1]
        through_a, through_b = (v[T - 1 :, :] for v in tall(ca, 2))
        last_a = jnp.sum(jnp.where(low_row, ends, 0.0), axis=1, keepdims=True) + through_a * jnp.sum(
            jnp.sum(inner[:HEAD], axis=0, keepdims=True), axis=1, keepdims=True
        )
        last_b = jnp.sum(jnp.where(low_row, 0.0, ends), axis=1, keepdims=True) + through_b * jnp.sum(
            jnp.sum(inner[HEAD:], axis=0, keepdims=True), axis=1, keepdims=True
        )
        dt_a, dt_b = tall(ca, 0)
        final = row[:, :1] == T - 1
        cum_ga = r[:T] - dt_a * q_a + jnp.where(final, last_a, 0.0)
        cum_gb = r[T:] - dt_b * q_b + jnp.where(final, last_b, 0.0)
        placed = jnp.where(
            lane == 0,
            q_a,
            jnp.where(
                lane == 1, q_b, jnp.where(lane == 32, cum_ga, jnp.where(lane == 33, cum_gb, 0.0))
            ),
        )
        acc[...] += pltpu.roll(placed, 2 * i, 1)
        d_pre = (dt_w * d_xt + skip_ref[:, at] * gy) * dsilu
        own = taps[3:4, :] * d_pre
        rim = jnp.zeros((8, 128), F32)
        for k in range(3):
            d = 3 - k
            z = pltpu.roll(taps[k : k + 1, :] * masks[k, 2 * T :] * d_pre, T - d, 0)
            own += jnp.where(row < T - d, z, 0.0)
            rim += jnp.where(row[T - 8 :] < T - d, 0.0, z[T - 8 :])
        dx_ref[:, at] = own.astype(BF)
        tail_ref[:, at] = own[T - 8 :]
        rim_ref[:, at] = rim
        return carry

    lax.fori_loop(0, pairs, pair, 0)

    ds = d_s[...]
    full_c = d_c[...] + dot(ds, bown[...], 1, 0, EXACT)
    full_b = d_b[...] + dot(ds, cown[...], 0, 0, EXACT)
    d_pre = jnp.concatenate([full_b, full_c], axis=1) * silu_bc[...]
    own = taps_b[3:4, :] * d_pre
    rim = jnp.zeros((8, 2 * STATE), F32)
    row2 = lax.broadcasted_iota(jnp.int32, (T, 2 * STATE), 0)
    for k in range(3):
        d = 3 - k
        z = pltpu.roll(taps_b[k : k + 1, :] * info[2 * T : 3 * T, k : k + 1] * d_pre, T - d, 0)
        own += jnp.where(row2 < T - d, z, 0.0)
        rim += jnp.where(row2[T - 8 :] < T - d, 0.0, z[T - 8 :])
    dbc_ref[...] = own
    rimbc_ref[...] = rim
    total = acc[...]
    d_log = pltpu.roll(dot(tri, total, 0, 0, EXACT), 96, 1)
    raw = raw_ref[2 * T : 3 * T, :]
    ddt_ref[...] = ((total - decay * d_log) * jax.nn.sigmoid(raw))[:, :32]


def ssm(xs, gs, bcs, raw, info, segrow, decay, skip, tapx, tapb):
    T, W = xs[0].shape
    vm = pltpu.VMEM
    return pl.pallas_call(
        ssm_kernel,
        out_shape=(
            jax.ShapeDtypeStruct((T, W), BF),
            jax.ShapeDtypeStruct((8, W), F32),
            jax.ShapeDtypeStruct((8, W), F32),
            jax.ShapeDtypeStruct((T, 2 * STATE), F32),
            jax.ShapeDtypeStruct((8, 2 * STATE), F32),
            jax.ShapeDtypeStruct((T, 32), F32),
        ),
        scratch_shapes=[
            vm((3, 3 * T, 128), F32), vm((T, T), F32), vm((T, T), F32), vm((T, 128), F32),
            vm((T, 128), F32), vm((128, T), F32), vm((2 * T, STATE), BF), vm((2 * T, STATE), BF),
            vm((T, STATE), F32), vm((T, STATE), F32), vm((T, 2 * STATE), F32),
            vm((T, T), F32), vm((T, STATE), F32), vm((T, STATE), F32), vm((T, 128), F32),
        ],
        compiler_params=pltpu.CompilerParams(vmem_limit_bytes=40 << 20),
        cost_estimate=pl.CostEstimate(
            flops=2 * 9 * T * 256 * W, bytes_accessed=8 * T * W * 2, transcendentals=6 * T * W
        ),
    )(*xs, *gs, *bcs, raw, info, segrow, decay, skip, tapx, tapb)


def on_device(
    hidden_in, w_bc, x_in, dt_raw, decay_rate, conv_x, conv_bc, skip_gain, span_len, grad_y
):
    T = x_in.shape[1]
    hidden = hidden_in[0]
    half_width = hidden.shape[1]
    n_ctx, n_fsdp, n_head = (lax.axis_size(a) for a in ("ctx", "fsdp", "head"))
    assert T * 2 == MOST and dt_raw.shape[2] == 32
    x0, g0, raw0 = x_in[0], grad_y[0], dt_raw[0]
    if n_fsdp == n_head:
        route = [(f * n_head + h, h * n_head + f) for f in range(n_fsdp) for h in range(n_head)]
        w_half = lax.ppermute(w_bc, ("fsdp", "head"), route)
    else:
        w_full = lax.all_gather(w_bc, "fsdp", axis=0, tiled=True)
        w_half = lax.dynamic_slice_in_dim(
            w_full, lax.axis_index("head") * half_width, half_width, 0
        )
    raws = [shifted(raw0, "ctx", d) for d in (2, 1)] + [raw0] + [shifted(raw0, "ctx", -d) for d in (1, 2)]
    x1, g1 = shifted(x0, "ctx", 1), shifted(g0, "ctx", -1)
    x2, g2 = shifted(x0, "ctx", 2), shifted(g0, "ctx", -2)

    swap = [(i, (i + 1) % n_head) for i in range(n_head)]
    partial_bc = jnp.dot(hidden, w_half, preferred_element_type=F32)
    bc_pre = (partial_bc + lax.ppermute(partial_bc, "head", swap)).astype(BF)
    bcs = [shifted(bc_pre, "ctx", d) for d in (2, 1)] + [bc_pre] + [shifted(bc_pre, "ctx", -d) for d in (1, 2)]

    n_blocks = n_ctx * n_fsdp
    blocks = hidden.reshape(T, n_blocks, half_width // n_blocks).transpose(1, 0, 2)
    hidden_all = lax.all_to_all(blocks, ("ctx", "fsdp"), 0, 0, tiled=True)

    position = (lax.axis_index("ctx") - 2) * T + jnp.arange(-3, 5 * T, dtype=jnp.int32)
    span_ends = jnp.cumsum(span_len[0])
    counted = jnp.sum((span_ends[None, :] <= position[:, None]).astype(jnp.int32), axis=1)
    segment = jnp.where(position >= 0, counted, -1).astype(F32)
    own_seg = segment[3:]
    by_block = own_seg.reshape(5, T)
    before = jnp.broadcast_to(segment[2 : 2 + 5 * T : T][:, None], (5, T)).reshape(-1)
    last = jnp.broadcast_to(by_block[:, T - 1 :], (5, T)).reshape(-1)
    info = jnp.stack(
        [(segment[k : k + 5 * T] == own_seg).astype(F32) for k in range(3)]
        + [(own_seg == before).astype(F32), (own_seg == last).astype(F32), own_seg],
        axis=1,
    )
    segrow = by_block[2:3]
    raw = jnp.tile(jnp.concatenate(raws), (1, 4))
    decay = jnp.tile(decay_rate, 4)[None, :]
    skip = jnp.repeat(skip_gain, HEAD)[None, :]

    dx, tail, rim, dbc, rimbc, ddt = ssm(
        (x2, x1, x0), (g0, g1, g2), bcs, raw, info, segrow, decay, skip, conv_x, conv_bc
    )
    back = shifted(rim, "ctx", -1)
    grad_x = lax.dynamic_update_slice(dx, (tail + back).astype(BF), (T - 8, 0))

    other = lax.ppermute(dbc, "head", swap)
    rim_same = shifted(rimbc, "ctx", -1)
    cross = [
        (c * n_head + h, (c - 1) * n_head + (h + 1) % n_head)
        for c in range(1, n_ctx)
        for h in range(n_head)
    ]
    rim_cross = lax.ppermute(rimbc, ("ctx", "head"), cross)
    d_bc = ((dbc + other) + jnp.pad(rim_same + rim_cross, ((T - 8, 0), (0, 0)))).astype(BF)
    grad_u = lax.dot_general(
        d_bc, w_half, (((1,), (1,)), ((), ())), preferred_element_type=F32
    ).astype(BF)
    d_all = lax.all_gather(d_bc, ("ctx", "fsdp"), axis=0)
    grad_w = lax.dot_general(
        hidden_all.reshape(n_blocks * T, -1),
        d_all.reshape(n_blocks * T, -1),
        (((0,), (0,)), ((), ())),
        preferred_element_type=F32,
    )
    return (grad_x[None], grad_u[None], ddt[None], grad_w[None])


def solution(mesh):
    return jax.shard_map(
        on_device,
        mesh=mesh,
        in_specs=(
            P(("groups", "fsdp"), "ctx", "head"),
            P("fsdp", None),
            P(("groups", "fsdp"), "ctx", "head"),
            P(("groups", "fsdp"), "ctx", "head"),
            P("head"),
            P(None, "head"),
            P(),
            P("head"),
            P(("groups", "fsdp"), None),
            P(("groups", "fsdp"), "ctx", "head"),
        ),
        out_specs=(
            P(("groups", "fsdp"), "ctx", "head"),
            P(("groups", "fsdp"), "ctx", "head"),
            P(("groups", "fsdp"), "ctx", "head"),
            P(("groups", "head"), ("ctx", "fsdp"), None),
        ),
        check_vma=False,
    )
```

time: 409 us -> 183 us (0.45)
  waiting for transfers between devices: 228 us -> 53.2 us
  matrix products: 52 us -> 7.1 us
  starting transfers between devices: 10.6 us -> 53.1 us
  other arithmetic: 40.1 us -> 1.02 us
  local copies, waits for them, and re-layouts: 38.2 us -> 11.7 us
  Pallas kernels: 0 us -> 21.5 us
  between operations: 17.4 us -> 1.09 us
  blocking collectives: 20.1 us -> 32.4 us
    all_gather x3 -> x0, waiting for transfers between devices: 164 us -> none  [the longest x2 108 us: entering(): everything = jax.tree.map(lambda part: lax.all_gather(part, axis), array)]
    reduce_scatter x1 -> x0, waiting for transfers between devices: 55.2 us -> none  [on_device(): lax.psum_scatter(lax.dot_general(hidden, d_bc, (((0,), (0,)), ((), ())),...]
    dot_general x25 -> x3, matrix products: 52 us -> 7.1 us  [the longest x1 3.37 us: on_device(): lax.dot_general(d_bc, w_half, (((1,), (1,)), ((), ())), preferred_element...]
    ppermute x4 -> x18, waiting for transfers between devices: 8.94 us -> 53.2 us  [the longest x14 52.6 us: shifted(): return lax.ppermute(block, axis, route)]
    ppermute x4 -> x18, starting transfers between devices: 10.4 us -> 48.8 us  [the longest x14 30.3 us: shifted(): return lax.ppermute(block, axis, route)]
    pallas_call x0 -> x1, Pallas kernels: none -> 21.5 us  [ssm(): pl.pallas_call(ssm_kernel, out_shape=(jax.ShapeDtypeStruct((T, W), BF), j...]
    all_gather x1, blocking collectives: 12.1 us -> 32.4 us  [on_device(): d_all = lax.all_gather(d_bc, ('ctx', 'fsdp'), axis=0)]
    select_n x9 -> x0, other arithmetic: 11.7 us -> none  [the longest x8 11.7 us: hop(): return jax.tree.map(lambda a, b: jnp.where(reached, a, b), new, before)]
  transfers between devices with their start and end apart: 8 -> 19, of which waited for: 8 -> 5; matrix products, arithmetic and copies ran while one was open for 16% -> 7% of each run, Pallas kernels for 0% -> 12%
where the time goes in v1:
time: 183 us; the launch traced here: 181 us
  waiting for transfers between devices  53.2 us (29%)
  starting transfers between devices  53.1 us (29%)
  blocking collectives  32.4 us (18%)
  Pallas kernels  21.5 us (12%)
  local copies, waits for them, and re-layouts  11.7 us (6%)
  matrix products  7.1 us (4%)
    ppermute x14, waiting for transfers between devices, shifted(): return lax.ppermute(block, axis, route)  52.6 us
    all_gather x1, blocking collectives, on_device(): d_all = lax.all_gather(d_bc, ('ctx', 'fsdp'), axis=0)  32.4 us
    ppermute x14, starting transfers between devices, shifted(): return lax.ppermute(block, axis, route)  30.3 us
    pallas_call x1, Pallas kernels, ssm(): pl.pallas_call(ssm_kernel, out_shape=(jax.ShapeDtypeStruct((T, W), BF), j...  21.5 us
    ppermute x1, starting transfers between devices, on_device(): w_half = lax.ppermute(w_bc, ('fsdp', 'head'), route)  17.1 us
    unnamed x29, local copies, waits for them, and re-layouts  6.55 us
    all_to_all x1, starting transfers between devices, on_device(): hidden_all = lax.all_to_all(blocks, ('ctx', 'fsdp'), 0, 0, tiled=True)  4.25 us
  transfers between devices with their start and end apart: 19, of which 5 were waited for; matrix products, arithmetic and copies ran while one was open for 7% of the time, Pallas kernels for 12%

profile of v1, /device:TPU:0, one launch (start us, length us, event | category | flops | bytes accessed | tf_op | source)
XLA Modules:
  0.0 181.1 jit_solution(15760956593541390286)
XLA Ops:
  0.6 17.1 %collective-permute-start.4 = (bf16[4096,256]{1,0:T(8,128)(2,1)}, bf16[4096,256]{1,0:T(8,128)(2,1)}, u32[]{:S(2)}, u32[]{:S(2)}) collective-permute-start(bf16[4096,256]{1,0:T(8,128)(2,1)} %param.11), channel_id=1, source_target_pairs={{0,0},{1,2},{2,1},{3,3},{4,4},{5,6},{6,5},{7,7},{8,8},{9,10},{10,9... | collective-permute-start | bytes 6291464 | tf_op jit(solution)/shard_map/ppermute | solution.py:251
  17.8 5.9 %collective-permute-start.10 = (f32[128,32]{0,1:T(8,128)}, f32[128,32]{0,1:T(8,128)S(1)}, u32[]{:S(2)}, u32[]{:S(2)}) collective-permute-start(f32[128,32]{0,1:T(8,128)} %bitcast.55), channel_id=1, source_target_pairs={{0,8},{4,12},{1,9},{5,13},{2,10},{6,14},{3,11},{7,15},{16,24},{20,... | collective-permute-start | bytes 49160 | tf_op jit(solution)/shard_map/ppermute | solution.py:19
  23.7 3.5 %collective-permute-start.11 = (f32[128,32]{0,1:T(8,128)}, f32[128,32]{0,1:T(8,128)S(1)}, u32[]{:S(2)}, u32[]{:S(2)}) collective-permute-start(f32[128,32]{0,1:T(8,128)} %bitcast.56), channel_id=1, source_target_pairs={{0,4},{4,8},{8,12},{1,5},{5,9},{9,13},{2,6},{6,10},{10,14},{3,7},{... | collective-permute-start | bytes 49160 | tf_op jit(solution)/shard_map/ppermute | solution.py:19
  27.2 1.3 collective-permute-start.12
  28.5 4.0 %collective-permute-start = (bf16[128,2048]{1,0:T(8,128)(2,1)}, bf16[128,2048]{1,0:T(8,128)(2,1)S(1)}, u32[]{:S(2)}, u32[]{:S(2)}) collective-permute-start(bf16[128,2048]{1,0:T(8,128)(2,1)} %bitcast.45), channel_id=1, source_target_pairs={{0,8},{4,12},{1,9},{5,13},{2,10},{6,14},{3,11},{7,15},{16,24},{20,... | collective-permute-start | bytes 1572872 | tf_op jit(solution)/shard_map/ppermute | solution.py:19
  32.5 2.3 %copy.51 = bf16[1,128,4096]{1,2,0:T(8,128)(2,1)} copy(bf16[1,128,4096]{2,1,0:T(8,128)(2,1)} %param.10) | data formatting | bytes 2097152 | tf_op args[0]
  34.8 2.4 %copy.52 = bf16[128,8,512]{2,0,1:T(8,128)(2,1)} copy(bf16[128,8,512]{0,2,1:T(8,128)(2,1)} %bitcast.52) | data formatting | bytes 2097152 | tf_op jit(solution)/shard_map/reshape;squeeze | solution.py:267
  37.2 4.3 %all-to-all-start = ((bf16[8,128,512]{2,1,0:T(8,128)(2,1)}), bf16[8,128,512]{2,1,0:T(8,128)(2,1)}, u32[]{:S(2)}, u32[]{:S(2)}) async-start(bf16[8,128,512]{2,1,0:T(8,128)(2,1)} %bitcast.51), calls=%async_computation | async-start | bytes 2097152 | tf_op jit(solution)/shard_map/all_to_all | solution.py:268
  42.9 3.8 %collective-permute-start.1 = (bf16[128,2048]{1,0:T(8,128)(2,1)S(1)}, bf16[128,2048]{1,0:T(8,128)(2,1)S(1)}, u32[]{:S(2)}, u32[]{:S(2)}) collective-permute-start(bf16[128,2048]{1,0:T(8,128)(2,1)S(1)} %bitcast.46), channel_id=1, source_target_pairs={{0,4},{4,8},{8,12},{1,5},{5,9},{9,13},{2,6},{6,10},{10,14},{3,7},{... | collective-permute-start | bytes 1572872 | tf_op jit(solution)/shard_map/ppermute | solution.py:19
  46.7 1.3 collective-permute-start.2
  48.0 1.3 collective-permute-start.3
  49.4 2.1 %fusion.1 = f32[128,256]{1,0:T(8,128)S(1)} fusion(bf16[4096,256]{1,0:T(8,128)(2,1)} %collective-permute-done.4, bf16[1,128,4096]{2,1,0:T(8,128)(2,1)S(1)} %copy-done.6), kind=kOutput, calls=%fused_computation.3 | convolution fusion | flops 268435456 | bytes 3276800 | tf_op jit(solution)/shard_map/dot_general | solution.py:262
  52.8 1.3 collective-permute-start.13
  54.2 45.3 %collective-permute-done.13 = f32[128,32]{0,1:T(8,128)S(1)} collective-permute-done((f32[128,32]{0,1:T(8,128)S(1)}, f32[128,32]{0,1:T(8,128)S(1)}, u32[]{:S(2)}, u32[]{:S(2)}) %collective-permute-start.13) | collective-permute-done | bytes 16416 | tf_op jit(solution)/shard_map/ppermute | solution.py:19
  99.5 1.4 collective-permute-start.6
  100.9 1.3 collective-permute-start.7
  102.2 1.3 collective-permute-start.8
  103.5 0.8 copy-done.2
  104.3 1.3 collective-permute-start.9
  106.4 1.1 copy.49.raw_ref
  107.5 1.3 collective-permute-done.8.b3
  108.8 2.6 %collective-permute-done.9.b4 = bf16[128,256]{1,0:T(8,128)(2,1)S(1)} collective-permute-done((bf16[128,256]{1,0:T(8,128)(2,1)S(1)}, bf16[128,256]{1,0:T(8,128)(2,1)S(1)}, u32[]{:S(2)}, u32[]{:S(2)}) %collective-permute-start.9) | collective-permute-done | bytes 65568 | tf_op jit(solution)/shard_map/ppermute | solution.py:19
  111.4 1.0 copy-done.3
  112.4 21.5 %shard_map.129 = (bf16[128,2048]{1,0:T(8,128)(2,1)}, f32[8,2048]{1,0:T(8,128)S(1)}, f32[8,2048]{1,0:T(8,128)S(1)}, f32[128,256]{1,0:T(8,128)S(1)}, f32[8,256]{1,0:T(8,128)S(1)}, /*index=5*/f32[128,32]{1,0:T(8,128)S(1)}) custom-call(bf16[128,2048]{1,0:T(8,128)(2,1)S(1)} %collective-permute-done.x2, bf16[128,2048]{1,0:T(8,128)(2,1)S(1)} %collective-permute-done.1.x1, ...), custom_call_target="tpu_custom_call" | custom-call | flops 1207959552 | bytes 4194304 | tf_op jit(solution)/shard_map/pallas_call | solution.py:217
  133.9 1.3 collective-permute-start.14
  135.2 1.3 collective-permute-start.16
  136.5 1.3 collective-permute-start.17
  138.6 3.4 %collective-permute-done.16 = f32[8,256]{1,0:T(8,128)S(1)} collective-permute-done((f32[8,256]{1,0:T(8,128)S(1)}, f32[8,256]{1,0:T(8,128)S(1)}, u32[]{:S(2)}, u32[]{:S(2)}) %collective-permute-start.16) | collective-permute-done | bytes 8224 | tf_op jit(solution)/shard_map/ppermute | solution.py:19
  142.7 32.4 %all-gather = bf16[1024,256]{1,0:T(8,128)(2,1)S(1)} all-gather(bf16[128,256]{1,0:T(8,128)(2,1)S(1)} %add_convert_fusion), channel_id=2, replica_groups=mesh['groups'=2,'ctx'=4,'fsdp'=2,'head'=2] {'ctx','fsdp'}, dimensions={0}, use_global_device_ids=true | all-gather | bytes 589824 | tf_op jit(solution)/shard_map/all_gather | solution.py:306
  175.1 1.7 convolution_bitcast_fusion
  176.7 1.0 copy.55
  177.7 3.4 %fusion = bf16[1,128,4096]{2,1,0:T(8,128)(2,1)} fusion(bf16[128,256]{1,0:T(8,128)(2,1)S(1)} %add_convert_fusion, bf16[4096,256]{1,0:T(8,128)(2,1)} %collective-permute-done.4), kind=kOutput, calls=%fused_computation.1 | convolution fusion | flops 268959744 | bytes 3211264 | tf_op jit(solution)/shard_map/dot_general | solution.py:303
  (69 shorter events, 4.9 us)
Async XLA Ops:
  0.6 47.4 %collective-permute-start.4 = (bf16[4096,256]{1,0:T(8,128)(2,1)}, bf16[4096,256]{1,0:T(8,128)(2,1)}, u32[]{:S(2)}, u32[]{:S(2)}) collective-permute-start(bf16[4096,256]{1,0:T(8,128)(2,1)} %param.11), channel_id=1, source_target_pairs={{0,0},{1,2},{2,1},{3,3},{4,4},{5,6},{6,5},{7,7},{8,8},{9,10},{10,9... | collective-permute-start | bytes 6291464 | tf_op jit(solution)/shard_map/ppermute | solution.py:251
  17.8 25.1 %collective-permute-start.10 = (f32[128,32]{0,1:T(8,128)}, f32[128,32]{0,1:T(8,128)S(1)}, u32[]{:S(2)}, u32[]{:S(2)}) collective-permute-start(f32[128,32]{0,1:T(8,128)} %bitcast.55), channel_id=1, source_target_pairs={{0,8},{4,12},{1,9},{5,13},{2,10},{6,14},{3,11},{7,15},{16,24},{20,... | collective-permute-start | bytes 49160 | tf_op jit(solution)/shard_map/ppermute | solution.py:19
  23.7 23.0 %collective-permute-start.11 = (f32[128,32]{0,1:T(8,128)}, f32[128,32]{0,1:T(8,128)S(1)}, u32[]{:S(2)}, u32[]{:S(2)}) collective-permute-start(f32[128,32]{0,1:T(8,128)} %bitcast.56), channel_id=1, source_target_pairs={{0,4},{4,8},{8,12},{1,5},{5,9},{9,13},{2,6},{6,10},{10,14},{3,7},{... | collective-permute-start | bytes 49160 | tf_op jit(solution)/shard_map/ppermute | solution.py:19
  27.2 24.2 %collective-permute-start.12 = (f32[128,32]{0,1:T(8,128)}, f32[128,32]{0,1:T(8,128)}, u32[]{:S(2)}, u32[]{:S(2)}) collective-permute-start(f32[128,32]{0,1:T(8,128)} %bitcast.57), channel_id=1, source_target_pairs={{4,0},{8,4},{12,8},{5,1},{9,5},{13,9},{6,2},{10,6},{14,10},{7,3},{... | collective-permute-start | bytes 49160 | tf_op jit(solution)/shard_map/ppermute | solution.py:19
  28.5 72.4 %collective-permute-start = (bf16[128,2048]{1,0:T(8,128)(2,1)}, bf16[128,2048]{1,0:T(8,128)(2,1)S(1)}, u32[]{:S(2)}, u32[]{:S(2)}) collective-permute-start(bf16[128,2048]{1,0:T(8,128)(2,1)} %bitcast.45), channel_id=1, source_target_pairs={{0,8},{4,12},{1,9},{5,13},{2,10},{6,14},{3,11},{7,15},{16,24},{20,... | collective-permute-start | bytes 1572872 | tf_op jit(solution)/shard_map/ppermute | solution.py:19
  34.8 6.7 %copy-start.10 = (s32[1,4]{1,0:T(1,128)S(1)}, s32[1,4]{1,0:T(1,128)}, u32[]{:S(2)}) copy-start(s32[1,4]{1,0:T(1,128)} %param.18) | copy-start | bytes 52
  34.8 7.8 %copy-start.8 = (f32[32]{0:T(128)S(1)}, f32[32]{0:T(128)}, u32[]{:S(2)}) copy-start(f32[32]{0:T(128)} %param.17) | copy-start | bytes 388
  34.8 8.0 %copy-start.9 = (f32[32]{0:T(128)S(1)}, f32[32]{0:T(128)}, u32[]{:S(2)}) copy-start(f32[32]{0:T(128)} %param.14) | copy-start | bytes 388
  34.8 8.1 %copy-start = (bf16[1,128,2048]{2,1,0:T(8,128)(2,1)S(1)}, bf16[1,128,2048]{2,1,0:T(8,128)(2,1)}, u32[]{:S(2)}) copy-start(bf16[1,128,2048]{2,1,0:T(8,128)(2,1)} %param.12) | copy-start | bytes 1572868
  34.8 11.9 %copy-start.1 = (bf16[1,128,2048]{2,1,0:T(8,128)(2,1)S(1)}, bf16[1,128,2048]{2,1,0:T(8,128)(2,1)}, u32[]{:S(2)}) copy-start(bf16[1,128,2048]{2,1,0:T(8,128)(2,1)} %param.19) | copy-start | bytes 1572868
  34.8 14.5 %copy-start.6 = (bf16[1,128,4096]{2,1,0:T(8,128)(2,1)S(1)}, bf16[1,128,4096]{2,1,0:T(8,128)(2,1)}, u32[]{:S(2)}) copy-start(bf16[1,128,4096]{2,1,0:T(8,128)(2,1)} %param.10) | copy-start | bytes 3145732
  37.2 137.8 %all-to-all-start = ((bf16[8,128,512]{2,1,0:T(8,128)(2,1)}), bf16[8,128,512]{2,1,0:T(8,128)(2,1)}, u32[]{:S(2)}, u32[]{:S(2)}) async-start(bf16[8,128,512]{2,1,0:T(8,128)(2,1)} %bitcast.51), calls=%async_computation | async-start | bytes 2097152 | tf_op jit(solution)/shard_map/all_to_all | solution.py:268
  41.5 10.0 %copy-start.7 = (f32[1,128,32]{1,2,0:T(8,128)S(1)}, f32[1,128,32]{1,2,0:T(8,128)}, u32[]{:S(2)}) copy-start(f32[1,128,32]{1,2,0:T(8,128)} %param.13) | copy-start | bytes 49156
  42.9 59.4 %collective-permute-start.1 = (bf16[128,2048]{1,0:T(8,128)(2,1)S(1)}, bf16[128,2048]{1,0:T(8,128)(2,1)S(1)}, u32[]{:S(2)}, u32[]{:S(2)}) collective-permute-start(bf16[128,2048]{1,0:T(8,128)(2,1)S(1)} %bitcast.46), channel_id=1, source_target_pairs={{0,4},{4,8},{8,12},{1,5},{5,9},{9,13},{2,6},{6,10},{10,14},{3,7},{... | collective-permute-start | bytes 1572872 | tf_op jit(solution)/shard_map/ppermute | solution.py:19
  46.7 56.8 %collective-permute-start.2 = (bf16[128,2048]{1,0:T(8,128)(2,1)S(1)}, bf16[128,2048]{1,0:T(8,128)(2,1)S(1)}, u32[]{:S(2)}, u32[]{:S(2)}) collective-permute-start(bf16[128,2048]{1,0:T(8,128)(2,1)S(1)} %bitcast.48), channel_id=1, source_target_pairs={{4,0},{8,4},{12,8},{5,1},{9,5},{13,9},{6,2},{10,6},{14,10},{7,3},{... | collective-permute-start | bytes 1572872 | tf_op jit(solution)/shard_map/ppermute | solution.py:19
  48.0 63.4 %copy-start.4 = (f32[4,2048]{1,0:T(4,128)S(1)}, f32[4,2048]{1,0:T(4,128)}, u32[]{:S(2)}) copy-start(f32[4,2048]{1,0:T(4,128)} %tapx_ref.1) | copy-start | bytes 98308
  48.0 63.4 %copy-start.5 = (f32[4,256]{1,0:T(4,128)S(1)}, f32[4,256]{1,0:T(4,128)}, u32[]{:S(2)}) copy-start(f32[4,256]{1,0:T(4,128)} %tapb_ref.1) | copy-start | bytes 12292
  48.0 59.5 %collective-permute-start.3 = (bf16[128,2048]{1,0:T(8,128)(2,1)S(1)}, bf16[128,2048]{1,0:T(8,128)(2,1)}, u32[]{:S(2)}, u32[]{:S(2)}) collective-permute-start(bf16[128,2048]{1,0:T(8,128)(2,1)S(1)} %bitcast.49), channel_id=1, source_target_pairs={{8,0},{12,4},{9,1},{13,5},{10,2},{14,6},{11,3},{15,7},{24,16},{28,... | collective-permute-start | bytes 1572872 | tf_op jit(solution)/shard_map/ppermute | solution.py:19
  51.4 1.4 collective-permute-start.5
  52.8 46.6 %collective-permute-start.13 = (f32[128,32]{0,1:T(8,128)S(1)}, f32[128,32]{0,1:T(8,128)S(1)}, u32[]{:S(2)}, u32[]{:S(2)}) collective-permute-start(f32[128,32]{0,1:T(8,128)S(1)} %bitcast.58), channel_id=1, source_target_pairs={{8,0},{12,4},{9,1},{13,5},{10,2},{14,6},{11,3},{15,7},{24,16},{28,... | collective-permute-start | bytes 49160 | tf_op jit(solution)/shard_map/ppermute | solution.py:19
  99.5 8.1 %collective-permute-start.6 = (bf16[128,256]{1,0:T(8,128)(2,1)S(1)}, bf16[128,256]{1,0:T(8,128)(2,1)S(1)}, u32[]{:S(2)}, u32[]{:S(2)}) collective-permute-start(bf16[128,256]{1,0:T(8,128)(2,1)S(1)} %add_convert_fusion.1.b0), channel_id=1, source_target_pairs={{0,8},{4,12},{1,9},{5,13},{2,10},{6,14},{3,11},{7,15},{16,24},{20,... | collective-permute-start | bytes 196616 | tf_op jit(solution)/shard_map/ppermute | solution.py:19
  100.9 6.6 %collective-permute-start.7 = (bf16[128,256]{1,0:T(8,128)(2,1)S(1)}, bf16[128,256]{1,0:T(8,128)(2,1)S(1)}, u32[]{:S(2)}, u32[]{:S(2)}) collective-permute-start(bf16[128,256]{1,0:T(8,128)(2,1)S(1)} %add_convert_fusion.1.b0), channel_id=1, source_target_pairs={{0,4},{4,8},{8,12},{1,5},{5,9},{9,13},{2,6},{6,10},{10,14},{3,7},{... | collective-permute-start | bytes 196616 | tf_op jit(solution)/shard_map/ppermute | solution.py:19
  102.2 6.6 %collective-permute-start.8 = (bf16[128,256]{1,0:T(8,128)(2,1)S(1)}, bf16[128,256]{1,0:T(8,128)(2,1)S(1)}, u32[]{:S(2)}, u32[]{:S(2)}) collective-permute-start(bf16[128,256]{1,0:T(8,128)(2,1)S(1)} %add_convert_fusion.1.b0), channel_id=1, source_target_pairs={{4,0},{8,4},{12,8},{5,1},{9,5},{13,9},{6,2},{10,6},{14,10},{7,3},{... | collective-permute-start | bytes 196616 | tf_op jit(solution)/shard_map/ppermute | solution.py:19
  103.5 0.8 copy-start.2
  104.3 7.0 %collective-permute-start.9 = (bf16[128,256]{1,0:T(8,128)(2,1)S(1)}, bf16[128,256]{1,0:T(8,128)(2,1)S(1)}, u32[]{:S(2)}, u32[]{:S(2)}) collective-permute-start(bf16[128,256]{1,0:T(8,128)(2,1)S(1)} %add_convert_fusion.1.b0), channel_id=1, source_target_pairs={{8,0},{12,4},{9,1},{13,5},{10,2},{14,6},{11,3},{15,7},{24,16},{28,... | collective-permute-start | bytes 196616 | tf_op jit(solution)/shard_map/ppermute | solution.py:19
  111.4 1.0 copy-start.3
  133.9 8.1 %collective-permute-start.14 = (f32[8,2048]{1,0:T(8,128)S(1)}, f32[8,2048]{1,0:T(8,128)S(1)}, u32[]{:S(2)}, u32[]{:S(2)}) collective-permute-start(f32[8,2048]{1,0:T(8,128)S(1)} %get-tuple-element.12), channel_id=1, source_target_pairs={{4,0},{8,4},{12,8},{5,1},{9,5},{13,9},{6,2},{10,6},{14,10},{7,3},{... | collective-permute-start | bytes 196616 | tf_op jit(solution)/shard_map/ppermute | solution.py:19
  135.2 6.8 %collective-permute-start.16 = (f32[8,256]{1,0:T(8,128)S(1)}, f32[8,256]{1,0:T(8,128)S(1)}, u32[]{:S(2)}, u32[]{:S(2)}) collective-permute-start(f32[8,256]{1,0:T(8,128)S(1)} %get-tuple-element.14), channel_id=1, source_target_pairs={{4,0},{8,4},{12,8},{5,1},{9,5},{13,9},{6,2},{10,6},{14,10},{7,3},{... | collective-permute-start | bytes 24584 | tf_op jit(solution)/shard_map/ppermute | solution.py:19
  136.5 5.5 %collective-permute-start.17 = (f32[8,256]{1,0:T(8,128)S(1)}, f32[8,256]{1,0:T(8,128)S(1)}, u32[]{:S(2)}, u32[]{:S(2)}) collective-permute-start(f32[8,256]{1,0:T(8,128)S(1)} %get-tuple-element.14), channel_id=1, source_target_pairs={{4,1},{5,0},{8,5},{9,4},{12,9},{13,8},{6,3},{7,2},{10,7},{11,6},{1... | collective-permute-start | bytes 24584 | tf_op jit(solution)/shard_map/ppermute | solution.py:301
  137.8 4.8 %collective-permute-start.15 = (f32[128,256]{1,0:T(8,128)S(1)}, f32[128,256]{1,0:T(8,128)S(1)}, u32[]{:S(2)}, u32[]{:S(2)}) collective-permute-start(f32[128,256]{1,0:T(8,128)S(1)} %get-tuple-element.13), channel_id=1, source_target_pairs={{0,1},{1,0},{2,3},{3,2},{4,5},{5,4},{6,7},{7,6},{8,9},{9,8},{10,11... | collective-permute-start | bytes 393224 | tf_op jit(solution)/shard_map/ppermute | solution.py:294

commit v2 on v1

--- a/solution.py
+++ b/solution.py
@@ -25,8 +25,39 @@
     )
 
 
-def ssm_kernel(
-    x2, x1, x0, g0, g1, g2, b2, b1, b0, b3, b4, raw_ref, info_ref, segrow_ref,
+def ssm_setup(T, c, span_ref, masks, bias_ref):
+    spans = span_ref.shape[1]
+    ends, total = [], 0
+    for i in range(spans):
+        total = total + span_ref[0, i]
+        ends.append(total)
+
+    def segment(p):
+        count = sum((e <= p).astype(jnp.int32) if hasattr(p, "shape") and p.shape else jnp.where(e <= p, 1, 0) for e in ends)
+        return jnp.where(p >= 0, count, -1)
+
+    iota = lax.broadcasted_iota(jnp.int32, (T, 1), 0)
+    taps, alive, last_same = [[], [], []], [], []
+    for j in range(5):
+        base = (c - 2 + j) * T
+        pos = base + iota
+        own = segment(pos)
+        for k in range(3):
+            taps[k].append((segment(pos - 3 + k) == own).astype(F32))
+        alive.append((own == segment(base - 1)).astype(F32))
+        last_same.append((own == segment(base + T - 1)).astype(F32))
+    for k in range(3):
+        masks[k] = jnp.broadcast_to(jnp.concatenate(taps[k][:3]), (3 * T, 128))
+    row_pos = c * T + lax.broadcasted_iota(jnp.int32, (1, T), 1)
+    same = segment(c * T + iota) == segment(row_pos)
+    row = lax.broadcasted_iota(jnp.int32, (T, T), 0)
+    lane = lax.broadcasted_iota(jnp.int32, (T, T), 1)
+    bias_ref[...] = jnp.where(same & (row >= lane), 0.0, -1e30)
+    return [jnp.concatenate(t) for t in taps], alive, last_same
+
+
+def ssm_body(
+    setup, x2, x1, x0, g0, g1, g2, b2, b1, b0, b3, b4, raw_ref,
     decay_ref, skip_ref, tapx_ref, tapb_ref,
     dx_ref, tail_ref, rim_ref, dbc_ref, rimbc_ref, ddt_ref,
     masks, bias_ref, s_ref, cols_a, cols_b, cum_rows, bprev, cnext, bown, cown,
@@ -38,24 +69,18 @@
     row = lax.broadcasted_iota(jnp.int32, (T, 128), 0)
     low = lane < HEAD
     group = lane // 32
-    info = info_ref[...]
-    for k in range(3):
-        masks[k] = jnp.broadcast_to(info[: 3 * T, k : k + 1], (3 * T, 128))
-
-    def col(block, k):
-        return info[block * T : (block + 1) * T, k : k + 1]
-
+    tap_masks, alive, last_same = setup
     tri = (row >= lane).astype(F32)
-    decay = decay_ref[...]
+    decay = jnp.concatenate([decay_ref[...]] * 4, axis=1)
     dts, cums, carried, toward = [], [], [], []
     for j in range(5):
-        raw = raw_ref[j * T : (j + 1) * T, :]
+        raw = raw_ref[j]
         dt = jnp.maximum(raw, 0.0) + jnp.log1p(jnp.exp(-jnp.abs(raw)))
         cum = dot(tri, -dt * decay, 1, 0, EXACT)
         dts.append(dt)
         cums.append(cum)
-        carried.append(jnp.exp(cum) * col(j, 3))
-        toward.append(jnp.exp(cum[T - 1 :, :] - cum) * col(j, 4))
+        carried.append(jnp.exp(cum) * alive[j])
+        toward.append(jnp.exp(cum[T - 1 :, :] - cum) * last_same[j])
     a1 = dts[1] * toward[1]
     a2 = dts[0] * toward[0] * carried[1][T - 1 :, :]
     c1 = carried[3]
@@ -67,14 +92,12 @@
     cols_a[...] = packed(dts[2], cums[2], carried[2], toward[2])
     cols_b[...] = packed(a2, a1, c1, c2)
     cum_rows[...] = cums[2].T
-    same = col(2, 5) == segrow_ref[...]
-    bias_ref[...] = jnp.where(same & (row >= lane), 0.0, -1e30)
 
     taps_b = tapb_ref[...]
     bc = jnp.concatenate([b2[...], b1[...], b0[...], b3[...], b4[...]]).astype(F32)
     pre_bc = taps_b[3:4, :] * bc
     for k in range(3):
-        pre_bc += taps_b[k : k + 1, :] * pltpu.roll(bc, 3 - k, 0) * info[:, k : k + 1]
+        pre_bc += taps_b[k : k + 1, :] * pltpu.roll(bc, 3 - k, 0) * tap_masks[k]
     sig_bc = jax.nn.sigmoid(pre_bc)
     conv_bc = pre_bc * sig_bc
     own_sig = sig_bc[2 * T : 3 * T]
@@ -176,7 +199,7 @@
             ),
         )
         acc[...] += pltpu.roll(placed, 2 * i, 1)
-        d_pre = (dt_w * d_xt + skip_ref[:, at] * gy) * dsilu
+        d_pre = (dt_w * d_xt + jnp.where(low_row, skip_ref[2 * i], skip_ref[2 * i + 1]) * gy) * dsilu
         own = taps[3:4, :] * d_pre
         rim = jnp.zeros((8, 128), F32)
         for k in range(3):
@@ -200,22 +223,42 @@
     row2 = lax.broadcasted_iota(jnp.int32, (T, 2 * STATE), 0)
     for k in range(3):
         d = 3 - k
-        z = pltpu.roll(taps_b[k : k + 1, :] * info[2 * T : 3 * T, k : k + 1] * d_pre, T - d, 0)
+        z = pltpu.roll(taps_b[k : k + 1, :] * tap_masks[k][2 * T : 3 * T] * d_pre, T - d, 0)
         own += jnp.where(row2 < T - d, z, 0.0)
         rim += jnp.where(row2[T - 8 :] < T - d, 0.0, z[T - 8 :])
     dbc_ref[...] = own
     rimbc_ref[...] = rim
     total = acc[...]
     d_log = pltpu.roll(dot(tri, total, 0, 0, EXACT), 96, 1)
-    raw = raw_ref[2 * T : 3 * T, :]
+    raw = raw_ref[2]
     ddt_ref[...] = ((total - decay * d_log) * jax.nn.sigmoid(raw))[:, :32]
 
 
-def ssm(xs, gs, bcs, raw, info, segrow, decay, skip, tapx, tapb):
+def ssm_scratch(T):
+    vm = pltpu.VMEM
+    return [
+        vm((3, 3 * T, 128), F32), vm((T, T), F32), vm((T, T), F32), vm((T, 128), F32),
+        vm((T, 128), F32), vm((128, T), F32), vm((2 * T, STATE), BF), vm((2 * T, STATE), BF),
+        vm((T, STATE), F32), vm((T, STATE), F32), vm((T, 2 * STATE), F32),
+        vm((T, T), F32), vm((T, STATE), F32), vm((T, STATE), F32), vm((T, 128), F32),
+    ]
+
+
+SMEM = pl.BlockSpec(memory_space=pltpu.SMEM)
+VMEM = pl.BlockSpec(memory_space=pltpu.VMEM)
+ANY = pl.BlockSpec(memory_space=pl.ANY)
+
+
+def local_kernel(span_ref, *refs):
+    setup = ssm_setup(refs[0].shape[0], lax.axis_index("ctx"), span_ref, *refs[22:24])
+    ssm_body(setup, *refs)
+
+
+def ssm(span, xs, gs, bcs, raw, decay, skip, tapx, tapb):
     T, W = xs[0].shape
-    vm = pltpu.VMEM
     return pl.pallas_call(
-        ssm_kernel,
+        local_kernel,
+        in_specs=[SMEM] + [VMEM] * 13 + [SMEM] + [VMEM] * 2,
         out_shape=(
             jax.ShapeDtypeStruct((T, W), BF),
             jax.ShapeDtypeStruct((8, W), F32),
@@ -224,17 +267,243 @@
             jax.ShapeDtypeStruct((8, 2 * STATE), F32),
             jax.ShapeDtypeStruct((T, 32), F32),
         ),
+        scratch_shapes=ssm_scratch(T),
+        compiler_params=pltpu.CompilerParams(vmem_limit_bytes=40 << 20),
+    )(span, *xs, *gs, *bcs, raw, decay, skip, tapx, tapb)
+
+
+def fused_kernel(
+    sizes, span_ref, skip_ref, hidden, w_bc, x_in, g_in, raw_in, decay_ref, tapx_ref, tapb_ref,
+    dx_ref, du_ref, ddt_ref, dw_ref,
+    hid_v, w_v, xbuf, gbuf, raws, bcs, part, part_in, tail, rim, rim_in, dbc, dbc_in,
+    rimbc, rimbc_in, hid_slots, d_slots, local_sem, send, recv, *scratch
+):
+    n_ctx, n_fsdp, n_head = sizes
+    c, f, h = (lax.axis_index(a) for a in ("ctx", "fsdp", "head"))
+    T, W = x_in.shape
+    half = hidden.shape[1]
+    n_blocks = n_ctx * n_fsdp
+    cols = half // n_blocks
+    block = c * n_fsdp + f
+    n_all = n_blocks * n_head
+    me = block * n_head + h
+    parts = 4
+    step = W // parts
+
+    barrier = pltpu.get_barrier_semaphore()
+    for o in range(1, n_all):
+        to = (me + o) % n_all
+        pl.semaphore_signal(
+            barrier, inc=1,
+            device_id={"ctx": to // (n_fsdp * n_head), "fsdp": (to // n_head) % n_fsdp, "head": to % n_head},
+            device_id_type=pl.DeviceIdType.MESH,
+        )
+
+    def remote(src, dst, k, **where):
+        return pltpu.make_async_remote_copy(
+            src_ref=src, dst_ref=dst, send_sem=send.at[k], recv_sem=recv.at[k],
+            device_id=where, device_id_type=pl.DeviceIdType.MESH,
+        )
+
+    diagonal = f == h
+    w_remote = remote(w_bc, w_v, 0, fsdp=h, head=f)
+    w_local = pltpu.make_async_copy(w_bc, w_v, local_sem.at[0])
+    loads = [
+        pltpu.make_async_copy(hidden, hid_v, local_sem.at[1]),
+        pltpu.make_async_copy(x_in, xbuf.at[2], local_sem.at[2]),
+        pltpu.make_async_copy(g_in, gbuf.at[0], local_sem.at[3]),
+        pltpu.make_async_copy(
+            hidden.at[:, pl.ds(pl.multiple_of(block * cols, 128), cols)],
+            hid_slots.at[0], local_sem.at[4],
+        ),
+    ]
+    for load in loads:
+        load.start()
+    raws[2] = jnp.concatenate([raw_in[...]] * 4, axis=1)
+    pl.semaphore_wait(barrier, n_all - 1)
+
+    @pl.when(jnp.logical_not(diagonal))
+    def _():
+        w_remote.start()
+
+    @pl.when(diagonal)
+    def _():
+        w_local.start()
+
+    def span_of(p):
+        return pl.ds(p * step, step)
+
+    def hop1(p):
+        return (
+            remote(x_in.at[:, span_of(p)], xbuf.at[1, :, span_of(p)], 1 + p, ctx=c + 1),
+            remote(g_in.at[:, span_of(p)], gbuf.at[1, :, span_of(p)], 5 + p, ctx=c - 1),
+        )
+
+    def hop2(p):
+        return (
+            remote(xbuf.at[1, :, span_of(p)], xbuf.at[0, :, span_of(p)], 9 + p, ctx=c + 1),
+            remote(gbuf.at[1, :, span_of(p)], gbuf.at[2, :, span_of(p)], 13 + p, ctx=c - 1),
+        )
+
+    def small(buf, base):
+        return [remote(buf.at[2], buf.at[2 - d], base + n, ctx=c + d) for n, d in enumerate((1, 2, -1, -2))]
+
+    def sends(d):
+        return (c + d >= 0) & (c + d < n_ctx)
+
+    def gets(d):
+        return (c - d >= 0) & (c - d < n_ctx)
+
+    offsets = (1, 2, -1, -2)
+    raw_copies, bc_copies = small(raws, 17), small(bcs, 21)
+    for copy, d in zip(raw_copies, offsets):
+        pl.when(sends(d))(copy.start)
+    for p in range(parts):
+        for copy, d in zip(hop1(p), (1, -1)):
+            pl.when(sends(d))(copy.start)
+
+    for d in offsets:
+
+        @pl.when(jnp.logical_not(gets(d)))
+        def _(d=d):
+            raws[2 - d] = jnp.zeros_like(raws[2])
+            bcs[2 - d] = jnp.zeros((T, 2 * STATE), BF)
+            if d > 0:
+                xbuf[2 - d] = jnp.zeros((T, W), BF)
+            else:
+                gbuf[-d] = jnp.zeros((T, W), BF)
+
+    setup = ssm_setup(T, c, span_ref, *scratch[:2])
+
+    for p in range(parts):
+        for one, two, d in zip(hop1(p), hop2(p), (1, -1)):
+            pl.when(gets(d))(one.wait_recv)
+            pl.when(gets(d) & sends(d))(two.start)
+    for load in loads:
+        load.wait()
+    pl.when(jnp.logical_not(diagonal))(w_remote.wait_recv)
+    pl.when(diagonal)(w_local.wait)
+
+    total = jnp.zeros((T, 2 * STATE), F32)
+    for k in range(0, half, 512):
+        total += dot(hid_v[:, k : k + 512], w_v[k : k + 512, :], 1, 0)
+    part[...] = total
+    swap_part = remote(part, part_in, 25, head=1 - h)
+    swap_part.start()
+    swap_part.wait_recv()
+    bcs[2] = (part[...] + part_in[...]).astype(BF)
+    for copy, d in zip(bc_copies, offsets):
+        pl.when(sends(d))(copy.start)
+
+    def spread(src, slots, base):
+        out = []
+        for o in range(1, n_blocks):
+            to = (block + o) % n_blocks
+            out.append(remote(src(to), slots.at[o], base + o, ctx=to // n_fsdp, fsdp=to % n_fsdp))
+        return out
+
+    for copies in (raw_copies, bc_copies):
+        for copy, d in zip(copies, offsets):
+            pl.when(gets(d))(copy.wait_recv)
+    for p in range(parts):
+        for copy, d in zip(hop2(p), (2, -2)):
+            pl.when(gets(d))(copy.wait_recv)
+    hid_copies = spread(
+        lambda to: hidden.at[:, pl.ds(pl.multiple_of(to * cols, 128), cols)], hid_slots, 31
+    )
+    for copy in hid_copies:
+        copy.start()
+
+    ssm_body(
+        setup, xbuf.at[0], xbuf.at[1], xbuf.at[2], gbuf.at[0], gbuf.at[1], gbuf.at[2],
+        *(bcs.at[j] for j in range(5)), raws, decay_ref, skip_ref, tapx_ref, tapb_ref,
+        dx_ref, tail, rim, dbc, rimbc, ddt_ref, *scratch
+    )
+
+    swap_d = remote(dbc, dbc_in, 26, head=1 - h)
+    rim_a = remote(rimbc, rimbc_in.at[0], 27, ctx=c - 1)
+    rim_b = remote(rimbc, rimbc_in.at[1], 28, ctx=c - 1, head=1 - h)
+    rim_x = remote(rim, rim_in, 29, ctx=c - 1)
+    swap_d.start()
+    for copy in (rim_a, rim_b, rim_x):
+        pl.when(sends(-1))(copy.start)
+
+    @pl.when(jnp.logical_not(gets(-1)))
+    def _():
+        rimbc_in[...] = jnp.zeros_like(rimbc_in)
+        rim_in[...] = jnp.zeros_like(rim_in)
+
+    swap_d.wait_recv()
+    for copy in (rim_a, rim_b):
+        pl.when(gets(-1))(copy.wait_recv)
+    d_sum = dbc[...] + dbc_in[...]
+    edge = d_sum[T - 8 :] + (rimbc_in[0] + rimbc_in[1])
+    d_bc = jnp.concatenate([d_sum[: T - 8], edge]).astype(BF)
+    d_slots[0] = d_bc
+    d_copies = spread(lambda to: d_slots.at[0], d_slots, 31 + n_blocks)
+    for copy in d_copies:
+        copy.start()
+    for k in range(0, half, 512):
+        du_ref[:, k : k + 512] = dot(d_bc, w_v[k : k + 512, :], 1, 1).astype(BF)
+    pl.when(gets(-1))(rim_x.wait_recv)
+    dx_ref[T - 16 :, :] = jnp.concatenate(
+        [dx_ref[T - 16 : T - 8, :].astype(F32), tail[...] + rim_in[...]]
+    ).astype(BF)
+    for copy in hid_copies + d_copies:
+        copy.wait_recv()
+    left = hid_slots[...].reshape(n_blocks * T, cols)
+    right = d_slots[...].reshape(n_blocks * T, 2 * STATE)
+    dw_ref[...] = dot(left, right, 0, 0)
+
+    pl.when(jnp.logical_not(diagonal))(w_remote.wait_send)
+    for p in range(parts):
+        for one, two, d in zip(hop1(p), hop2(p), (1, -1)):
+            pl.when(sends(d))(one.wait_send)
+            pl.when(gets(d) & sends(d))(two.wait_send)
+    for copies in (raw_copies, bc_copies):
+        for copy, d in zip(copies, offsets):
+            pl.when(sends(d))(copy.wait_send)
+    swap_part.wait_send()
+    swap_d.wait_send()
+    for copy in (rim_a, rim_b, rim_x):
+        pl.when(sends(-1))(copy.wait_send)
+    for copy in hid_copies + d_copies:
+        copy.wait_send()
+
+
+def fused(sizes, span, skip, hidden, w_bc, x, g, raw, decay, tapx, tapb):
+    T, W = x.shape
+    half = hidden.shape[1]
+    n_blocks = sizes[0] * sizes[1]
+    cols = half // n_blocks
+    vm = pltpu.VMEM
+    n_sem = 31 + 2 * n_blocks
+    return pl.pallas_call(
+        lambda *refs: fused_kernel(sizes, *refs),
+        in_specs=[SMEM, SMEM, ANY, ANY, ANY, ANY, VMEM, VMEM, VMEM, VMEM],
+        out_specs=[VMEM] * 4,
+        out_shape=(
+            jax.ShapeDtypeStruct((T, W), BF),
+            jax.ShapeDtypeStruct((T, half), BF),
+            jax.ShapeDtypeStruct((T, 32), F32),
+            jax.ShapeDtypeStruct((cols, 2 * STATE), F32),
+        ),
         scratch_shapes=[
-            vm((3, 3 * T, 128), F32), vm((T, T), F32), vm((T, T), F32), vm((T, 128), F32),
-            vm((T, 128), F32), vm((128, T), F32), vm((2 * T, STATE), BF), vm((2 * T, STATE), BF),
-            vm((T, STATE), F32), vm((T, STATE), F32), vm((T, 2 * STATE), F32),
-            vm((T, T), F32), vm((T, STATE), F32), vm((T, STATE), F32), vm((T, 128), F32),
-        ],
-        compiler_params=pltpu.CompilerParams(vmem_limit_bytes=40 << 20),
-        cost_estimate=pl.CostEstimate(
-            flops=2 * 9 * T * 256 * W, bytes_accessed=8 * T * W * 2, transcendentals=6 * T * W
+            vm((T, half), BF), vm((half, 2 * STATE), BF), vm((3, T, W), BF), vm((3, T, W), BF),
+            vm((5, T, 128), F32), vm((5, T, 2 * STATE), BF),
+            vm((T, 2 * STATE), F32), vm((T, 2 * STATE), F32),
+            vm((8, W), F32), vm((8, W), F32), vm((8, W), F32),
+            vm((T, 2 * STATE), F32), vm((T, 2 * STATE), F32),
+            vm((8, 2 * STATE), F32), vm((2, 8, 2 * STATE), F32),
+            vm((n_blocks, T, cols), BF), vm((n_blocks, T, 2 * STATE), BF),
+            pltpu.SemaphoreType.DMA((5,)),
+            pltpu.SemaphoreType.DMA((n_sem,)),
+            pltpu.SemaphoreType.DMA((n_sem,)),
+        ] + ssm_scratch(T),
+        compiler_params=pltpu.CompilerParams(
+            vmem_limit_bytes=48 << 20, collective_id=0, has_side_effects=True
         ),
-    )(*xs, *gs, *bcs, raw, info, segrow, decay, skip, tapx, tapb)
+    )(span, skip, hidden, w_bc, x, g, raw, decay, tapx, tapb)
 
 
 def on_device(
@@ -244,71 +513,44 @@
     hidden = hidden_in[0]
     half_width = hidden.shape[1]
     n_ctx, n_fsdp, n_head = (lax.axis_size(a) for a in ("ctx", "fsdp", "head"))
+    n_blocks = n_ctx * n_fsdp
     assert T * 2 == MOST and dt_raw.shape[2] == 32
     x0, g0, raw0 = x_in[0], grad_y[0], dt_raw[0]
-    if n_fsdp == n_head:
-        route = [(f * n_head + h, h * n_head + f) for f in range(n_fsdp) for h in range(n_head)]
-        w_half = lax.ppermute(w_bc, ("fsdp", "head"), route)
-    else:
-        w_full = lax.all_gather(w_bc, "fsdp", axis=0, tiled=True)
-        w_half = lax.dynamic_slice_in_dim(
-            w_full, lax.axis_index("head") * half_width, half_width, 0
-        )
-    raws = [shifted(raw0, "ctx", d) for d in (2, 1)] + [raw0] + [shifted(raw0, "ctx", -d) for d in (1, 2)]
-    x1, g1 = shifted(x0, "ctx", 1), shifted(g0, "ctx", -1)
-    x2, g2 = shifted(x0, "ctx", 2), shifted(g0, "ctx", -2)
-
+    decay = decay_rate[None, :]
+    if n_fsdp == 2 and n_head == 2 and (half_width // n_blocks) % 128 == 0:
+        dx, du, ddt, dw = fused(
+            (n_ctx, n_fsdp, n_head), span_len, skip_gain, hidden, w_bc, x0, g0, raw0, decay,
+            conv_x, conv_bc,
+        )
+        return (dx[None], du[None], ddt[None], dw[None])
+    w_full = lax.all_gather(w_bc, "fsdp", axis=0, tiled=True)
+    w_half = lax.dynamic_slice_in_dim(w_full, lax.axis_index("head") * half_width, half_width, 0)
+
+    def around(v):
+        return [shifted(v, "ctx", d) for d in (2, 1)] + [v] + [shifted(v, "ctx", -d) for d in (1, 2)]
+
+    raw = jnp.tile(jnp.stack(around(raw0)), (1, 1, 4))
+    x2, x1 = shifted(x0, "ctx", 2), shifted(x0, "ctx", 1)
+    g1, g2 = shifted(g0, "ctx", -1), shifted(g0, "ctx", -2)
     swap = [(i, (i + 1) % n_head) for i in range(n_head)]
     partial_bc = jnp.dot(hidden, w_half, preferred_element_type=F32)
     bc_pre = (partial_bc + lax.ppermute(partial_bc, "head", swap)).astype(BF)
-    bcs = [shifted(bc_pre, "ctx", d) for d in (2, 1)] + [bc_pre] + [shifted(bc_pre, "ctx", -d) for d in (1, 2)]
-
-    n_blocks = n_ctx * n_fsdp
     blocks = hidden.reshape(T, n_blocks, half_width // n_blocks).transpose(1, 0, 2)
     hidden_all = lax.all_to_all(blocks, ("ctx", "fsdp"), 0, 0, tiled=True)
-
-    position = (lax.axis_index("ctx") - 2) * T + jnp.arange(-3, 5 * T, dtype=jnp.int32)
-    span_ends = jnp.cumsum(span_len[0])
-    counted = jnp.sum((span_ends[None, :] <= position[:, None]).astype(jnp.int32), axis=1)
-    segment = jnp.where(position >= 0, counted, -1).astype(F32)
-    own_seg = segment[3:]
-    by_block = own_seg.reshape(5, T)
-    before = jnp.broadcast_to(segment[2 : 2 + 5 * T : T][:, None], (5, T)).reshape(-1)
-    last = jnp.broadcast_to(by_block[:, T - 1 :], (5, T)).reshape(-1)
-    info = jnp.stack(
-        [(segment[k : k + 5 * T] == own_seg).astype(F32) for k in range(3)]
-        + [(own_seg == before).astype(F32), (own_seg == last).astype(F32), own_seg],
-        axis=1,
-    )
-    segrow = by_block[2:3]
-    raw = jnp.tile(jnp.concatenate(raws), (1, 4))
-    decay = jnp.tile(decay_rate, 4)[None, :]
-    skip = jnp.repeat(skip_gain, HEAD)[None, :]
-
     dx, tail, rim, dbc, rimbc, ddt = ssm(
-        (x2, x1, x0), (g0, g1, g2), bcs, raw, info, segrow, decay, skip, conv_x, conv_bc
+        span_len, (x2, x1, x0), (g0, g1, g2), around(bc_pre), raw, decay, skip_gain, conv_x, conv_bc
     )
     back = shifted(rim, "ctx", -1)
     grad_x = lax.dynamic_update_slice(dx, (tail + back).astype(BF), (T - 8, 0))
-
-    other = lax.ppermute(dbc, "head", swap)
-    rim_same = shifted(rimbc, "ctx", -1)
-    cross = [
-        (c * n_head + h, (c - 1) * n_head + (h + 1) % n_head)
-        for c in range(1, n_ctx)
-        for h in range(n_head)
-    ]
-    rim_cross = lax.ppermute(rimbc, ("ctx", "head"), cross)
-    d_bc = ((dbc + other) + jnp.pad(rim_same + rim_cross, ((T - 8, 0), (0, 0)))).astype(BF)
+    mine = dbc + jnp.pad(shifted(rimbc, "ctx", -1), ((T - 8, 0), (0, 0)))
+    d_bc = (mine + lax.ppermute(mine, "head", swap)).astype(BF)
     grad_u = lax.dot_general(
         d_bc, w_half, (((1,), (1,)), ((), ())), preferred_element_type=F32
     ).astype(BF)
     d_all = lax.all_gather(d_bc, ("ctx", "fsdp"), axis=0)
     grad_w = lax.dot_general(
-        hidden_all.reshape(n_blocks * T, -1),
-        d_all.reshape(n_blocks * T, -1),
-        (((0,), (0,)), ((), ())),
-        preferred_element_type=F32,
+        hidden_all.reshape(n_blocks * T, -1), d_all.reshape(n_blocks * T, -1),
+        (((0,), (0,)), ((), ())), preferred_element_type=F32,
     )
     return (grad_x[None], grad_u[None], ddt[None], grad_w[None])
 

time: 183 us -> 86.8 us (0.47)
  the two profiles are of different devices: /device:TPU:0 before, /device:TPU:11 now
where the time goes in v2:
time: 86.8 us; the launch traced here: 86.3 us
  Pallas kernels  74.9 us (86%)
  local copies, waits for them, and re-layouts  10.8 us (12%)
    pallas_call x1, Pallas kernels, fused(): pl.pallas_call(lambda *refs: fused_kernel(sizes, *refs), in_specs=[SMEM,...  74.9 us
    unnamed x21, local copies, waits for them, and re-layouts  10.8 us

profile of v2, /device:TPU:11, one launch (start us, length us, event | category | flops | bytes accessed | tf_op | source)
XLA Modules:
  0.0 86.3 jit_solution(10662908965992212019)
XLA Ops:
  0.6 0.8 copy.14
  1.4 0.0 copy-start
  1.5 1.2 %copy-done = bf16[1,128,4096]{2,1,0:T(8,128)(2,1)S(1)} copy-done((bf16[1,128,4096]{2,1,0:T(8,128)(2,1)S(1)}, bf16[1,128,4096]{2,1,0:T(8,128)(2,1)}, u32[]{:S(2)}) %copy-start) | copy-done | bytes 1048600
  2.7 0.0 copy-start.1
  2.7 1.0 %copy-done.1 = bf16[1,128,2048]{2,1,0:T(8,128)(2,1)S(1)} copy-done((bf16[1,128,2048]{2,1,0:T(8,128)(2,1)S(1)}, bf16[1,128,2048]{2,1,0:T(8,128)(2,1)}, u32[]{:S(2)}) %copy-start.1) | copy-done | bytes 524312
  3.7 0.0 copy-start.2
  3.7 1.0 %copy-done.2 = bf16[1,128,2048]{2,1,0:T(8,128)(2,1)S(1)} copy-done((bf16[1,128,2048]{2,1,0:T(8,128)(2,1)S(1)}, bf16[1,128,2048]{2,1,0:T(8,128)(2,1)}, u32[]{:S(2)}) %copy-start.2) | copy-done | bytes 524312
  4.8 0.0 copy-start.3
  4.8 0.8 copy-done.3
  5.5 0.0 copy-start.4
  5.5 0.7 copy-done.4
  6.2 0.0 copy-start.5
  6.2 0.7 copy-done.5
  6.9 0.0 copy-start.6
  6.9 0.7 copy-done.6
  7.5 0.0 copy-start.7
  7.5 0.7 copy-done.7
  8.2 74.9 %shard_map.129 = (bf16[128,2048]{1,0:T(8,128)(2,1)S(1)}, bf16[128,4096]{1,0:T(8,128)(2,1)S(1)}, f32[128,32]{1,0:T(8,128)S(1)}, f32[512,256]{1,0:T(8,128)S(1)}) custom-call(s32[1,4]{1,0:T(1,128)S(1)} %copy-done.5, f32[32]{0:T(128)S(1)} %copy-done.6, bf16[128,4096]{1,0:T(8,128)(2,1)S(1)} %bitcast.10, bf16[4096,256]{1,0:T(8,128)(2,1)} %refs_3_.1, ...), custom_call_target="tpu_custom_call" | custom-call | tf_op jit(solution)/shard_map/pallas_call | solution.py:481
  83.1 0.7 copy.15
  83.8 0.8 copy.19
  84.6 1.0 %copy.20 = bf16[1,128,4096]{2,1,0:T(8,128)(2,1)} copy(bf16[1,128,4096]{2,1,0:T(8,128)(2,1)S(1)} %bitcast.9) | data formatting | bytes 2097152
  85.5 0.8 copy.21
Async XLA Ops:
  1.4 1.2 %copy-start = (bf16[1,128,4096]{2,1,0:T(8,128)(2,1)S(1)}, bf16[1,128,4096]{2,1,0:T(8,128)(2,1)}, u32[]{:S(2)}) copy-start(bf16[1,128,4096]{2,1,0:T(8,128)(2,1)} %param.10) | copy-start | bytes 3145732
  2.7 1.0 %copy-start.1 = (bf16[1,128,2048]{2,1,0:T(8,128)(2,1)S(1)}, bf16[1,128,2048]{2,1,0:T(8,128)(2,1)}, u32[]{:S(2)}) copy-start(bf16[1,128,2048]{2,1,0:T(8,128)(2,1)} %param.12) | copy-start | bytes 1572868
  3.7 1.0 %copy-start.2 = (bf16[1,128,2048]{2,1,0:T(8,128)(2,1)S(1)}, bf16[1,128,2048]{2,1,0:T(8,128)(2,1)}, u32[]{:S(2)}) copy-start(bf16[1,128,2048]{2,1,0:T(8,128)(2,1)} %param.19) | copy-start | bytes 1572868
  4.8 0.8 copy-start.3
  5.5 0.7 copy-start.4
  6.2 0.7 copy-start.5
  6.9 0.7 copy-start.6
  7.5 0.7 copy-start.7

commit v3 on v2

--- a/solution.py
+++ b/solution.py
@@ -8,6 +8,8 @@
 STATE = 128
 HEAD = 64
 MOST = 256
+W_PARTS = 4
+PARTS = 4
 BF = jnp.bfloat16
 F32 = jnp.float32
 EXACT = lax.Precision.HIGHEST
@@ -57,7 +59,7 @@
 
 
 def ssm_body(
-    setup, x2, x1, x0, g0, g1, g2, b2, b1, b0, b3, b4, raw_ref,
+    gate, setup, x2, x1, x0, g0, g1, g2, b2, b1, b0, b3, b4, raw_ref,
     decay_ref, skip_ref, tapx_ref, tapb_ref,
     dx_ref, tail_ref, rim_ref, dbc_ref, rimbc_ref, ddt_ref,
     masks, bias_ref, s_ref, cols_a, cols_b, cum_rows, bprev, cnext, bown, cown,
@@ -212,7 +214,11 @@
         rim_ref[:, at] = rim
         return carry
 
-    lax.fori_loop(0, pairs, pair, 0)
+    def some(p, carry):
+        gate(p)
+        return lax.fori_loop(p * (pairs // PARTS), (p + 1) * (pairs // PARTS), pair, carry)
+
+    lax.fori_loop(0, PARTS, some, 0)
 
     ds = d_s[...]
     full_c = d_c[...] + dot(ds, bown[...], 1, 0, EXACT)
@@ -231,7 +237,7 @@
     total = acc[...]
     d_log = pltpu.roll(dot(tri, total, 0, 0, EXACT), 96, 1)
     raw = raw_ref[2]
-    ddt_ref[...] = ((total - decay * d_log) * jax.nn.sigmoid(raw))[:, :32]
+    ddt_ref[...] = ((total - decay * d_log) * jax.nn.sigmoid(raw)).T[:32]
 
 
 def ssm_scratch(T):
@@ -251,7 +257,7 @@
 
 def local_kernel(span_ref, *refs):
     setup = ssm_setup(refs[0].shape[0], lax.axis_index("ctx"), span_ref, *refs[22:24])
-    ssm_body(setup, *refs)
+    ssm_body(lambda p: None, setup, *refs)
 
 
 def ssm(span, xs, gs, bcs, raw, decay, skip, tapx, tapb):
@@ -265,7 +271,7 @@
             jax.ShapeDtypeStruct((8, W), F32),
             jax.ShapeDtypeStruct((T, 2 * STATE), F32),
             jax.ShapeDtypeStruct((8, 2 * STATE), F32),
-            jax.ShapeDtypeStruct((T, 32), F32),
+            jax.ShapeDtypeStruct((32, T), F32),
         ),
         scratch_shapes=ssm_scratch(T),
         compiler_params=pltpu.CompilerParams(vmem_limit_bytes=40 << 20),
@@ -273,12 +279,12 @@
 
 
 def fused_kernel(
-    sizes, span_ref, skip_ref, hidden, w_bc, x_in, g_in, raw_in, decay_ref, tapx_ref, tapb_ref,
+    sizes, span_any, skip_any, hidden, w_bc, x_in, g_in, raw_any, decay_any, tapx_any, tapb_any,
     dx_ref, du_ref, ddt_ref, dw_ref,
-    hid_v, w_v, xbuf, gbuf, raws, bcs, part, part_in, tail, rim, rim_in, dbc, dbc_in,
+    span_ref, skip_ref, raw_in, decay_ref, tapx_ref, tapb_ref, hid_v, w_v, xbuf, gbuf, raws, bcs, part, part_in, tail, rim, rim_in, dbc, dbc_in,
     rimbc, rimbc_in, hid_slots, d_slots, local_sem, send, recv, *scratch
 ):
-    n_ctx, n_fsdp, n_head = sizes
+    n_ctx, n_fsdp, n_head, n_groups = sizes
     c, f, h = (lax.axis_index(a) for a in ("ctx", "fsdp", "head"))
     T, W = x_in.shape
     half = hidden.shape[1]
@@ -287,7 +293,7 @@
     block = c * n_fsdp + f
     n_all = n_blocks * n_head
     me = block * n_head + h
-    parts = 4
+    parts = PARTS
     step = W // parts
 
     barrier = pltpu.get_barrier_semaphore()
@@ -299,6 +305,11 @@
             device_id_type=pl.DeviceIdType.MESH,
         )
 
+    pl.semaphore_signal(
+        barrier, inc=1, device_id={"groups": 1 - lax.axis_index("groups")},
+        device_id_type=pl.DeviceIdType.MESH,
+    )
+
     def remote(src, dst, k, **where):
         return pltpu.make_async_remote_copy(
             src_ref=src, dst_ref=dst, send_sem=send.at[k], recv_sem=recv.at[k],
@@ -306,8 +317,34 @@
         )
 
     diagonal = f == h
-    w_remote = remote(w_bc, w_v, 0, fsdp=h, head=f)
+    y = lax.axis_index("groups")
+    share = half // n_groups
+    piece = share // W_PARTS
+    base_sem = 31 + 2 * n_blocks
+
+    def w_rows(owner, q):
+        return pl.ds(pl.multiple_of(owner * share + q * piece, 128), piece)
+
+    def w_hop(q):
+        rows = w_rows(y, q)
+        return remote(w_bc.at[rows], w_v.at[rows], base_sem + q, fsdp=h, head=f)
+
+    def w_across(q, owner):
+        rows = w_rows(owner, q)
+        return remote(w_v.at[rows], w_v.at[rows], base_sem + W_PARTS + q, groups=1 - y)
+
     w_local = pltpu.make_async_copy(w_bc, w_v, local_sem.at[0])
+    first = [
+        pltpu.make_async_copy(src, dst, local_sem.at[5 + n])
+        for n, (src, dst) in enumerate(
+            (
+                (raw_any, raw_in), (span_any, span_ref), (skip_any, skip_ref),
+                (decay_any, decay_ref), (tapx_any, tapx_ref), (tapb_any, tapb_ref),
+            )
+        )
+    ]
+    for load in first:
+        load.start()
     loads = [
         pltpu.make_async_copy(hidden, hid_v, local_sem.at[1]),
         pltpu.make_async_copy(x_in, xbuf.at[2], local_sem.at[2]),
@@ -319,19 +356,19 @@
     ]
     for load in loads:
         load.start()
-    raws[2] = jnp.concatenate([raw_in[...]] * 4, axis=1)
-    pl.semaphore_wait(barrier, n_all - 1)
+    pl.semaphore_wait(barrier, n_all)
 
     @pl.when(jnp.logical_not(diagonal))
     def _():
-        w_remote.start()
+        for q in range(W_PARTS):
+            w_hop(q).start()
 
     @pl.when(diagonal)
     def _():
         w_local.start()
 
     def span_of(p):
-        return pl.ds(p * step, step)
+        return pl.ds(pl.multiple_of(p * step, 128), step)
 
     def hop1(p):
         return (
@@ -356,11 +393,14 @@
 
     offsets = (1, 2, -1, -2)
     raw_copies, bc_copies = small(raws, 17), small(bcs, 21)
-    for copy, d in zip(raw_copies, offsets):
-        pl.when(sends(d))(copy.start)
     for p in range(parts):
         for copy, d in zip(hop1(p), (1, -1)):
             pl.when(sends(d))(copy.start)
+    for load in first:
+        load.wait()
+    raws[2] = jnp.concatenate([raw_in[...]] * 4, axis=0).T
+    for copy, d in zip(raw_copies, offsets):
+        pl.when(sends(d))(copy.start)
 
     for d in offsets:
 
@@ -375,13 +415,25 @@
 
     setup = ssm_setup(T, c, span_ref, *scratch[:2])
 
-    for p in range(parts):
+    def forward(p):
         for one, two, d in zip(hop1(p), hop2(p), (1, -1)):
             pl.when(gets(d))(one.wait_recv)
             pl.when(gets(d) & sends(d))(two.start)
+
+    forward(0)
     for load in loads:
         load.wait()
-    pl.when(jnp.logical_not(diagonal))(w_remote.wait_recv)
+
+    @pl.when(jnp.logical_not(diagonal))
+    def _():
+        for q in range(W_PARTS):
+            w_hop(q).wait_recv()
+            if n_groups == 2:
+                w_across(q, y).start()
+        if n_groups == 2:
+            for q in range(W_PARTS):
+                w_across(q, 1 - y).wait_recv()
+
     pl.when(diagonal)(w_local.wait)
 
     total = jnp.zeros((T, 2 * STATE), F32)
@@ -394,6 +446,8 @@
     bcs[2] = (part[...] + part_in[...]).astype(BF)
     for copy, d in zip(bc_copies, offsets):
         pl.when(sends(d))(copy.start)
+    for p in range(1, parts):
+        forward(p)
 
     def spread(src, slots, base):
         out = []
@@ -405,17 +459,21 @@
     for copies in (raw_copies, bc_copies):
         for copy, d in zip(copies, offsets):
             pl.when(gets(d))(copy.wait_recv)
-    for p in range(parts):
+    hid_copies = spread(
+        lambda to: hidden.at[:, pl.ds(pl.multiple_of(to * cols, 128), cols)], hid_slots, 31
+    )
+
+    def gate(p):
         for copy, d in zip(hop2(p), (2, -2)):
             pl.when(gets(d))(copy.wait_recv)
-    hid_copies = spread(
-        lambda to: hidden.at[:, pl.ds(pl.multiple_of(to * cols, 128), cols)], hid_slots, 31
-    )
-    for copy in hid_copies:
-        copy.start()
+
+        @pl.when(p == 1)
+        def _():
+            for copy in hid_copies:
+                copy.start()
 
     ssm_body(
-        setup, xbuf.at[0], xbuf.at[1], xbuf.at[2], gbuf.at[0], gbuf.at[1], gbuf.at[2],
+        gate, setup, xbuf.at[0], xbuf.at[1], xbuf.at[2], gbuf.at[0], gbuf.at[1], gbuf.at[2],
         *(bcs.at[j] for j in range(5)), raws, decay_ref, skip_ref, tapx_ref, tapb_ref,
         dx_ref, tail, rim, dbc, rimbc, ddt_ref, *scratch
     )
@@ -455,7 +513,13 @@
     right = d_slots[...].reshape(n_blocks * T, 2 * STATE)
     dw_ref[...] = dot(left, right, 0, 0)
 
-    pl.when(jnp.logical_not(diagonal))(w_remote.wait_send)
+    @pl.when(jnp.logical_not(diagonal))
+    def _():
+        for q in range(W_PARTS):
+            w_hop(q).wait_send()
+            if n_groups == 2:
+                w_across(q, y).wait_send()
+
     for p in range(parts):
         for one, two, d in zip(hop1(p), hop2(p), (1, -1)):
             pl.when(sends(d))(one.wait_send)
@@ -477,18 +541,20 @@
     n_blocks = sizes[0] * sizes[1]
     cols = half // n_blocks
     vm = pltpu.VMEM
-    n_sem = 31 + 2 * n_blocks
+    n_sem = 31 + 2 * n_blocks + 2 * W_PARTS
     return pl.pallas_call(
         lambda *refs: fused_kernel(sizes, *refs),
-        in_specs=[SMEM, SMEM, ANY, ANY, ANY, ANY, VMEM, VMEM, VMEM, VMEM],
+        in_specs=[ANY] * 10,
         out_specs=[VMEM] * 4,
         out_shape=(
             jax.ShapeDtypeStruct((T, W), BF),
             jax.ShapeDtypeStruct((T, half), BF),
-            jax.ShapeDtypeStruct((T, 32), F32),
+            jax.ShapeDtypeStruct((32, T), F32),
             jax.ShapeDtypeStruct((cols, 2 * STATE), F32),
         ),
         scratch_shapes=[
+            pltpu.SMEM(span.shape, jnp.int32), pltpu.SMEM(skip.shape, F32), vm(raw.shape, F32),
+            vm(decay.shape, F32), vm(tapx.shape, F32), vm(tapb.shape, F32),
             vm((T, half), BF), vm((half, 2 * STATE), BF), vm((3, T, W), BF), vm((3, T, W), BF),
             vm((5, T, 128), F32), vm((5, T, 2 * STATE), BF),
             vm((T, 2 * STATE), F32), vm((T, 2 * STATE), F32),
@@ -496,12 +562,12 @@
             vm((T, 2 * STATE), F32), vm((T, 2 * STATE), F32),
             vm((8, 2 * STATE), F32), vm((2, 8, 2 * STATE), F32),
             vm((n_blocks, T, cols), BF), vm((n_blocks, T, 2 * STATE), BF),
-            pltpu.SemaphoreType.DMA((5,)),
+            pltpu.SemaphoreType.DMA((15,)),
             pltpu.SemaphoreType.DMA((n_sem,)),
             pltpu.SemaphoreType.DMA((n_sem,)),
         ] + ssm_scratch(T),
         compiler_params=pltpu.CompilerParams(
-            vmem_limit_bytes=48 << 20, collective_id=0, has_side_effects=True
+            vmem_limit_bytes=62 << 20, collective_id=0, has_side_effects=True
         ),
     )(span, skip, hidden, w_bc, x, g, raw, decay, tapx, tapb)
 
@@ -512,17 +578,19 @@
     T = x_in.shape[1]
     hidden = hidden_in[0]
     half_width = hidden.shape[1]
-    n_ctx, n_fsdp, n_head = (lax.axis_size(a) for a in ("ctx", "fsdp", "head"))
+    n_ctx, n_fsdp, n_head, n_groups = (
+        lax.axis_size(a) for a in ("ctx", "fsdp", "head", "groups")
+    )
     n_blocks = n_ctx * n_fsdp
     assert T * 2 == MOST and dt_raw.shape[2] == 32
     x0, g0, raw0 = x_in[0], grad_y[0], dt_raw[0]
     decay = decay_rate[None, :]
-    if n_fsdp == 2 and n_head == 2 and (half_width // n_blocks) % 128 == 0:
+    if n_fsdp == 2 and n_head == 2 and n_groups == 2 and (half_width // n_blocks) % 128 == 0:
         dx, du, ddt, dw = fused(
-            (n_ctx, n_fsdp, n_head), span_len, skip_gain, hidden, w_bc, x0, g0, raw0, decay,
+            (n_ctx, n_fsdp, n_head, n_groups), span_len, skip_gain, hidden, w_bc, x0, g0, raw0.T, decay,
             conv_x, conv_bc,
         )
-        return (dx[None], du[None], ddt[None], dw[None])
+        return (dx[None], du[None], ddt.T[None], dw[None])
     w_full = lax.all_gather(w_bc, "fsdp", axis=0, tiled=True)
     w_half = lax.dynamic_slice_in_dim(w_full, lax.axis_index("head") * half_width, half_width, 0)
 
@@ -552,7 +620,7 @@
         hidden_all.reshape(n_blocks * T, -1), d_all.reshape(n_blocks * T, -1),
         (((0,), (0,)), ((), ())), preferred_element_type=F32,
     )
-    return (grad_x[None], grad_u[None], ddt[None], grad_w[None])
+    return (grad_x[None], grad_u[None], ddt.T[None], grad_w[None])
 
 
 def solution(mesh):

time: 86.8 us -> 85.7 us (0.987)
  the two profiles are of different devices: /device:TPU:11 before, /device:TPU:0 now
where the time goes in v3:
time: 85.7 us; the launch traced here: 85.5 us
  Pallas kernels  79.2 us (92%)
  local copies, waits for them, and re-layouts  5.63 us (7%)
    pallas_call x1, Pallas kernels, fused(): pl.pallas_call(lambda *refs: fused_kernel(sizes, *refs), in_specs=[ANY] *...  79.2 us
    unnamed x8, local copies, waits for them, and re-layouts  5.63 us

profile of v3, /device:TPU:0, one launch (start us, length us, event | category | flops | bytes accessed | tf_op | source)
XLA Modules:
  0.0 85.5 jit_solution(1829036298670880944)
XLA Ops:
  0.6 79.2 %shard_map.129 = (bf16[128,2048]{1,0:T(8,128)(2,1)}, bf16[128,4096]{1,0:T(8,128)(2,1)}, f32[32,128]{1,0:T(8,128)}, f32[512,256]{1,0:T(8,128)}) custom-call(s32[1,4]{1,0:T(1,128)} %refs_0_.1, f32[32]{0:T(128)} %refs_1_.1, bf16[128,4096]{1,0:T(8,128)(2,1)} %bitcast.14, bf16[4096,256]{1,0:T(8,128)(2,1)} %refs_3_.1, bf16[128,2048]{1,0:T(8,128)(2,1)} %bitcast.15, ...), custom_call_target="tpu_custom_call" | custom-call | tf_op jit(solution)/shard_map/pallas_call | solution.py:545
  79.9 0.0 copy-start.1
  79.9 0.0 copy-start
  79.9 1.9 %copy.18 = bf16[1,128,2048]{2,1,0:T(8,128)(2,1)} copy(bf16[1,128,2048]{2,1,0:T(8,128)(2,1)} %bitcast.18) | data formatting | bytes 1048576
  81.8 2.3 %copy.19 = bf16[1,128,4096]{2,1,0:T(8,128)(2,1)} copy(bf16[1,128,4096]{2,1,0:T(8,128)(2,1)} %bitcast.13) | data formatting | bytes 2097152
  84.1 0.0 copy-done.1
  84.1 0.6 copy.20
  84.7 0.0 copy-done
  84.7 0.8 copy.21
Async XLA Ops:
  79.9 4.2 %copy-start.1 = (f32[32,128]{1,0:T(8,128)S(1)}, f32[32,128]{1,0:T(8,128)}, u32[]{:S(2)}) copy-start(f32[32,128]{1,0:T(8,128)} %get-tuple-element.10) | copy-start | bytes 49156
  79.9 4.8 %copy-start = (f32[512,256]{1,0:T(8,128)S(1)}, f32[512,256]{1,0:T(8,128)}, u32[]{:S(2)}) copy-start(f32[512,256]{1,0:T(8,128)} %get-tuple-element.11) | copy-start | bytes 1572868

commit v4 on v3

--- a/solution.py
+++ b/solution.py
@@ -8,8 +8,7 @@
 STATE = 128
 HEAD = 64
 MOST = 256
-W_PARTS = 4
-PARTS = 4
+W_PARTS = PARTS = 4
 BF = jnp.bfloat16
 F32 = jnp.float32
 EXACT = lax.Precision.HIGHEST
@@ -420,16 +419,19 @@
             pl.when(gets(d))(one.wait_recv)
             pl.when(gets(d) & sends(d))(two.start)
 
-    forward(0)
+    for q in range(parts):
+        forward(q)
+
+        @pl.when(jnp.logical_not(diagonal))
+        def _(q=q):
+            w_hop(q).wait_recv()
+            w_across(q, y).start()
+
     for load in loads:
         load.wait()
 
     @pl.when(jnp.logical_not(diagonal))
     def _():
-        for q in range(W_PARTS):
-            w_hop(q).wait_recv()
-            if n_groups == 2:
-                w_across(q, y).start()
         if n_groups == 2:
             for q in range(W_PARTS):
                 w_across(q, 1 - y).wait_recv()
@@ -446,9 +448,6 @@
     bcs[2] = (part[...] + part_in[...]).astype(BF)
     for copy, d in zip(bc_copies, offsets):
         pl.when(sends(d))(copy.start)
-    for p in range(1, parts):
-        forward(p)
-
     def spread(src, slots, base):
         out = []
         for o in range(1, n_blocks):
@@ -467,11 +466,8 @@
         for copy, d in zip(hop2(p), (2, -2)):
             pl.when(gets(d))(copy.wait_recv)
 
-        @pl.when(p == 1)
-        def _():
-            for copy in hid_copies:
-                copy.start()
-
+    for copy in hid_copies:
+        copy.start()
     ssm_body(
         gate, setup, xbuf.at[0], xbuf.at[1], xbuf.at[2], gbuf.at[0], gbuf.at[1], gbuf.at[2],
         *(bcs.at[j] for j in range(5)), raws, decay_ref, skip_ref, tapx_ref, tapb_ref,

time: 85.7 us -> 82.6 us (0.964)
  the two profiles are of different devices: /device:TPU:0 before, /device:TPU:30 now
where the time goes in v4:
time: 82.6 us; the launch traced here: 82.4 us
  Pallas kernels  76.1 us (92%)
  local copies, waits for them, and re-layouts  5.63 us (7%)
    pallas_call x1, Pallas kernels, fused(): pl.pallas_call(lambda *refs: fused_kernel(sizes, *refs), in_specs=[ANY] *...  76.1 us
    unnamed x8, local copies, waits for them, and re-layouts  5.63 us

profile of v4, /device:TPU:30, one launch (start us, length us, event | category | flops | bytes accessed | tf_op | source)
XLA Modules:
  0.0 82.4 jit_solution(12853884280590954063)
XLA Ops:
  0.6 76.1 %shard_map.129 = (bf16[128,2048]{1,0:T(8,128)(2,1)}, bf16[128,4096]{1,0:T(8,128)(2,1)}, f32[32,128]{1,0:T(8,128)}, f32[512,256]{1,0:T(8,128)}) custom-call(s32[1,4]{1,0:T(1,128)} %refs_0_.1, f32[32]{0:T(128)} %refs_1_.1, bf16[128,4096]{1,0:T(8,128)(2,1)} %bitcast.14, bf16[4096,256]{1,0:T(8,128)(2,1)} %refs_3_.1, bf16[128,2048]{1,0:T(8,128)(2,1)} %bitcast.15, ...), custom_call_target="tpu_custom_call" | custom-call | tf_op jit(solution)/shard_map/pallas_call | solution.py:541
  76.8 0.0 copy-start.1
  76.8 0.0 copy-start
  76.8 1.9 %copy.18 = bf16[1,128,2048]{2,1,0:T(8,128)(2,1)} copy(bf16[1,128,2048]{2,1,0:T(8,128)(2,1)} %bitcast.18) | data formatting | bytes 1048576
  78.7 2.3 %copy.19 = bf16[1,128,4096]{2,1,0:T(8,128)(2,1)} copy(bf16[1,128,4096]{2,1,0:T(8,128)(2,1)} %bitcast.13) | data formatting | bytes 2097152
  81.0 0.0 copy-done.1
  81.0 0.6 copy.20
  81.6 0.0 copy-done
  81.6 0.8 copy.21
Async XLA Ops:
  76.8 4.2 %copy-start.1 = (f32[32,128]{1,0:T(8,128)S(1)}, f32[32,128]{1,0:T(8,128)}, u32[]{:S(2)}) copy-start(f32[32,128]{1,0:T(8,128)} %get-tuple-element.10) | copy-start | bytes 49156
  76.8 4.8 %copy-start = (f32[512,256]{1,0:T(8,128)S(1)}, f32[512,256]{1,0:T(8,128)}, u32[]{:S(2)}) copy-start(f32[512,256]{1,0:T(8,128)} %get-tuple-element.11) | copy-start | bytes 1572868
